TPU v7x, 256 devices: a whole 4x4x8 slice. The times are simulated.
256 devices in a mesh: coil: 16 (over x_hi, y, core), slab: 16 (over x_lo, z).
Axes of the slice: x: 4 (x_hi: 2, x_lo: 2; x = x_hi * 2 + x_lo), y: 4, z: 8, core: 2. Of those that a mesh axis runs over, the one named last changes fastest.
Arguments:
- image: float32 [48, 2, 256, 256], P('coil', None, 'slab'), may hold values from -6 to 6
- sensitivity: bfloat16 [16, 48, 2, 256, 256], P('coil', None, None, 'slab'), may hold values from -1.1953125 to 1.1953125
- kspace: bfloat16 [16, 48, 2, 256, 256], P('coil', 'slab'), may hold values from -6 to 6
- sampling: int32 [256, 256], replicated, may hold values 0 or 1
- conv_in: bfloat16 [32, 2, 3, 3, 3], replicated, may hold values from -0.875 to 0.875
- conv_mid: bfloat16 [32, 32, 3, 3, 3], replicated, may hold values from -0.21875 to 0.21875
- conv_out: bfloat16 [2, 32, 3, 3, 3], replicated, may hold values from -0.21875 to 0.21875
Outputs:
- estimate: float32 [48, 2, 256, 256], P('coil', None, 'slab')
All inputs are finite; a program needn't handle non-finite values.
Results may differ from a plain program's by a relative error of at most 0.015.
Values may be sent and summed in bfloat16 or wider, within the bound.
No kernel may reach another device: no remote copies, remote signals or barrier semaphores. Data moves between devices by JAX's collectives and lax.ppermute only.
A program may use at most 64 MiB of HBM per device.

v0:
```python
import math

import jax
import jax.numpy as jnp
from jax import lax
from jax.sharding import PartitionSpec as P


def sent_to_all(array, axis):
    count = lax.axis_size(axis)
    return lax.all_to_all(
        jnp.broadcast_to(array[None], (count, *array.shape)), axis, 0, 0, tiled=True
    )


def joined_along(tiles, dim):
    tiles = jnp.moveaxis(tiles, 0, dim)
    shape = tiles.shape
    return tiles.reshape(*shape[:dim], shape[dim] * shape[dim + 1], *shape[dim + 2 :])


def collect(array, axis, dim):
    tiles = sent_to_all(array, axis)
    return joined_along(tiles, dim)


def in_blocks(array, dim, count):
    before, after = (array.shape[:dim], array.shape[dim + 1 :])
    return jnp.moveaxis(array.reshape(*before, count, -1, *after), dim, 0)


def summed_on_arrival(array, axis, dim):
    count = lax.axis_size(axis)
    tiles = lax.all_to_all(in_blocks(array, dim, count), axis, 0, 0, tiled=True)
    return jnp.sum(tiles.astype(jnp.float32), axis=0)


def with_halo(array, sides, width):
    for axis, dim in sides:
        count, length = (lax.axis_size(axis), array.shape[dim])
        up = [(i, (i + 1) % count) for i in range(count - 1)]
        down = [(j, i) for i, j in up]
        last = lax.slice_in_dim(array, length - width, length, axis=dim)
        first = lax.slice_in_dim(array, 0, width, axis=dim)
        before = lax.ppermute(last, axis, up)
        after = lax.ppermute(first, axis, down)
        array = jnp.concatenate([before, array, after], axis=dim)
    return array


def twiddle(length, sign):
    ramp = jnp.arange(length, dtype=jnp.int32)
    phases = ramp[:, None] * ramp[None, :] % length
    angles = phases.astype(jnp.float32) * (2.0 * math.pi / length)
    factor = 1.0 / math.sqrt(length)
    return jnp.concatenate(
        [jnp.cos(angles) * factor, sign * jnp.sin(angles) * factor], axis=1
    ).astype(jnp.bfloat16)


def transform_last(values, table):
    length = values.shape[-1]
    product = jnp.einsum("...czj,jk->...czk", values, table, preferred_element_type=jnp.float32)
    real_part = product[..., 0, :, :length] - product[..., 1, :, length:]
    imag_part = product[..., 0, :, length:] + product[..., 1, :, :length]
    return jnp.stack([real_part, imag_part], axis=-3)


def transform_middle(values, table):
    length = values.shape[-2]
    product = jnp.einsum("...cjy,jk->...cky", values, table, preferred_element_type=jnp.float32)
    real_part = product[..., 0, :length, :] - product[..., 1, length:, :]
    imag_part = product[..., 0, length:, :] + product[..., 1, :length, :]
    return jnp.stack([real_part, imag_part], axis=-3)


def times_map(maps, field):
    real_part = maps[..., 0, :, :] * field[..., 0, :, :] - maps[..., 1, :, :] * field[..., 1, :, :]
    imag_part = maps[..., 0, :, :] * field[..., 1, :, :] + maps[..., 1, :, :] * field[..., 0, :, :]
    return jnp.stack([real_part, imag_part], axis=-3)


def times_conj(maps, field):
    real_part = maps[..., 0, :, :] * field[..., 0, :, :] + maps[..., 1, :, :] * field[..., 1, :, :]
    imag_part = maps[..., 0, :, :] * field[..., 1, :, :] - maps[..., 1, :, :] * field[..., 0, :, :]
    return jnp.stack([real_part, imag_part], axis=-3)


def convolve(values, weights):
    return lax.conv_general_dilated(
        values[None],
        weights,
        (1, 1, 1),
        ((0, 0), (0, 0), (1, 1)),
        dimension_numbers=("NDCHW", "OIDHW", "NDCHW"),
        preferred_element_type=jnp.float32,
    )[0]


def local(image, sensitivity, kspace, sampling, conv_in, conv_mid, conv_out):
    brick_rows = image.shape[0]
    depth = image.shape[2]
    width_y = image.shape[3]
    lines_z = kspace.shape[3]
    forward_y = twiddle(width_y, -1.0)
    forward_z = twiddle(lines_z, -1.0)
    back_z = twiddle(lines_z, 1.0)
    back_y = twiddle(width_y, 1.0)
    maps = sensitivity.astype(jnp.float32)
    coil_image = times_map(
        maps, collect(image.astype(jnp.bfloat16), "coil", 0).astype(jnp.float32)
    ).astype(jnp.bfloat16)
    lifted = transform_last(coil_image, forward_y).astype(jnp.bfloat16)
    spectra = lax.all_to_all(lifted, "slab", split_axis=1, concat_axis=3, tiled=True)
    spectrum = transform_middle(spectra, forward_z)
    keep = sampling.astype(jnp.float32)
    misfit = (keep * (spectrum - kspace.astype(jnp.float32))).astype(jnp.bfloat16)
    returned = transform_middle(misfit, back_z).astype(jnp.bfloat16)
    slabs = lax.all_to_all(returned, "slab", split_axis=3, concat_axis=1, tiled=True)
    field = transform_last(slabs, back_y)
    maps = sensitivity.astype(jnp.float32)
    gradient = summed_on_arrival(
        jnp.sum(times_conj(maps, field), axis=0).astype(jnp.bfloat16), "coil", 0
    )
    halfway = image - gradient
    start_layer = halfway.astype(jnp.bfloat16)

    def inside(margin):
        place_x = (
            lax.axis_index("coil") * brick_rows
            - margin
            + jnp.arange(brick_rows + 2 * margin, dtype=jnp.int32)
        )
        place_z = (
            lax.axis_index("slab") * depth
            - margin
            + jnp.arange(depth + 2 * margin, dtype=jnp.int32)
        )
        valid_x = (place_x >= 0) & (place_x < brick_rows * lax.axis_size("coil"))
        valid_z = (place_z >= 0) & (place_z < depth * lax.axis_size("slab"))
        return (valid_x[:, None, None, None] & valid_z[None, None, :, None]).astype(jnp.float32)

    padded = with_halo(start_layer, (("coil", 0), ("slab", 2)), 3)
    first = (jax.nn.relu(convolve(padded, conv_in)) * inside(2)).astype(jnp.bfloat16)
    second = (jax.nn.relu(convolve(first, conv_mid)) * inside(1)).astype(jnp.bfloat16)
    correction = convolve(second, conv_out)
    return halfway + correction


def solution(mesh):
    return jax.shard_map(
        local,
        mesh=mesh,
        in_specs=(
            P("coil", None, "slab", None),
            P("coil", None, None, "slab", None),
            P("coil", "slab", None, None, None),
            P(),
            P(),
            P(),
            P(),
        ),
        out_specs=P("coil", None, "slab", None),
        check_vma=False,
    )
```

profile of v0, /device:TPU:4, one launch (start us, length us, event | category | flops | bytes accessed | tf_op | source)
XLA Modules:
  0.0 424.7 jit_solution(12881706801468067258)
XLA Ops:
  0.0 0.0 copy-start
  0.0 0.9 convert_element_type.98
  1.0 1.0 broadcast_in_dim.4
  1.9 7.5 %all-to-all-start = ((bf16[16,3,2,16,256]{4,3,1,2,0:T(8,128)(2,1)}), bf16[16,3,2,16,256]{4,3,1,2,0:T(8,128)(2,1)S(1)}, u32[]{:S(2)}, u32[]{:S(2)}) async-start(bf16[16,3,2,16,256]{4,3,1,2,0:T(8,128)(2,1)} %broadcast_in_dim.4), calls=%async_computation | async-start | bytes 1572864 | tf_op jit(solution)/shard_map/all_to_all | solution.py:11
  9.4 1.1 multiply_convert_fusion.2
  10.5 1.4 copy_convert_fusion
  11.9 9.8 %all-to-all-done = bf16[16,3,2,16,256]{4,3,1,2,0:T(8,128)(2,1)S(1)} async-done(((bf16[16,3,2,16,256]{4,3,1,2,0:T(8,128)(2,1)}), bf16[16,3,2,16,256]{4,3,1,2,0:T(8,128)(2,1)S(1)}, u32[]{:S(2)}, u32[]{:S(2)}) %all-to-all-start) | async-done | bytes 786464 | tf_op jit(solution)/shard_map/all_to_all | solution.py:11
  21.7 0.2 copy.51
  21.9 0.5 fusion.44
  22.4 0.0 copy-start.6
  22.4 0.6 convolution_bitcast_fusion.3
  23.0 0.2 fusion.39
  23.2 1.0 maximum_bitcast_fusion
  24.1 9.2 %all-to-all-start.1 = ((bf16[1,48,2,16,256]{4,3,2,0,1:T(8,128)(2,1)}), bf16[1,48,2,16,256]{4,3,2,0,1:T(8,128)(2,1)S(1)}, u32[]{:S(2)}, u32[]{:S(2)}) async-start(bf16[1,48,2,16,256]{4,3,2,0,1:T(8,128)(2,1)} %maximum_bitcast_fusion), calls=%async_computation.1 | async-start | bytes 1572864 | tf_op jit(solution)/shard_map/all_to_all | solution.py:114
  33.3 1.0 multiply_convert_fusion.3
  34.3 20.7 %all-to-all-done.1 = bf16[1,48,2,16,256]{4,3,2,0,1:T(8,128)(2,1)S(1)} async-done(((bf16[1,48,2,16,256]{4,3,2,0,1:T(8,128)(2,1)}), bf16[1,48,2,16,256]{4,3,2,0,1:T(8,128)(2,1)S(1)}, u32[]{:S(2)}, u32[]{:S(2)}) %all-to-all-start.1) | async-done | bytes 786464 | tf_op jit(solution)/shard_map/all_to_all | solution.py:114
  55.0 0.1 copy.54
  55.1 0.6 convolution_bitcast_fusion.2
  55.7 0.2 slice_subtract_fusion.2
  55.9 0.2 copy-done.5
  56.2 0.7 convolution_bitcast_fusion.1
  56.8 0.2 fusion.37
  57.0 0.1 pad_maximum_fusion
  57.1 0.8 copy.57
  57.9 25.5 %all_to_all.40 = bf16[1,3,2,256,256]{4,2,1,0,3:T(2,128)(2,1)S(1)} all-to-all(bf16[1,3,2,256,256]{4,2,1,0,3:T(2,128)(2,1)S(1)} %copy.57), channel_id=1, replica_groups=mesh['coil'=16,'slab'=16] {'slab'}, dimensions={3} | all-to-all | bytes 1572864 | tf_op jit(solution)/shard_map/all_to_all | solution.py:119
  83.5 0.1 copy.76
  83.6 0.6 convolution_bitcast_fusion
  84.2 0.0 copy-start.3
  84.2 0.6 add_convert_fusion
  84.7 0.1 pad_maximum_fusion.1
  84.8 1.0 copy.60
  85.8 5.7 %all-to-all-start.3 = ((bf16[16,3,2,16,256]{4,3,1,2,0:T(8,128)(2,1)}), bf16[16,3,2,16,256]{4,3,1,2,0:T(8,128)(2,1)S(1)}, u32[]{:S(2)}, u32[]{:S(2)}) async-start(bf16[16,3,2,16,256]{4,3,1,2,0:T(8,128)(2,1)} %copy.60), calls=%async_computation.3 | async-start | bytes 1572864 | tf_op jit(solution)/shard_map/all_to_all | solution.py:34
  91.5 0.1 and_convert_fusion
  91.6 12.2 %all-to-all-done.3 = bf16[16,3,2,16,256]{4,3,1,2,0:T(8,128)(2,1)S(1)} async-done(((bf16[16,3,2,16,256]{4,3,1,2,0:T(8,128)(2,1)}), bf16[16,3,2,16,256]{4,3,1,2,0:T(8,128)(2,1)S(1)}, u32[]{:S(2)}, u32[]{:S(2)}) %all-to-all-start.3) | async-done | bytes 786464 | tf_op jit(solution)/shard_map/all_to_all | solution.py:34
  103.8 0.1 convert_reduce_fusion
  103.9 0.0 copy-start.1
  103.9 5.2 %collective-permute-start.1 = (bf16[3,2,16,256]{3,2,0,1:T(8,128)(2,1)S(1)}, bf16[3,2,16,256]{3,2,0,1:T(8,128)(2,1)S(1)}, u32[]{:S(2)}, u32[]{:S(2)}) collective-permute-start(bf16[3,2,16,256]{3,2,0,1:T(8,128)(2,1)S(1)} %fusion.59), channel_id=1, source_target_pairs={{16,0},{32,16},{48,32},{64,48},{80,64},{96,80},{112,96},{128,112},... | collective-permute-start | bytes 147464 | tf_op jit(solution)/shard_map/ppermute | solution.py:46
  109.2 1.9 collective-permute-start
  111.1 0.0 collective-permute-done.1
  111.1 7.1 %collective-permute-done = bf16[3,2,16,256]{3,2,0,1:T(8,128)(2,1)S(1)} collective-permute-done((bf16[3,2,16,256]{3,2,0,1:T(8,128)(2,1)S(1)}, bf16[3,2,16,256]{3,2,0,1:T(8,128)(2,1)S(1)}, u32[]{:S(2)}, u32[]{:S(2)}) %collective-permute-start) | collective-permute-done | bytes 49184 | tf_op jit(solution)/shard_map/ppermute | solution.py:45
  118.2 4.2 collective-permute-start.2
  122.5 1.3 collective-permute-start.3
  123.8 0.1 and_convert_fusion.1
  123.8 0.2 collective-permute-done.2
  124.1 4.2 collective-permute-done.3
  128.3 0.1 maximum_bitcast_fusion.1
  128.4 0.2 pad
  128.6 0.0 copy-start.7
  128.6 0.0 copy-start.9
  128.6 0.7 reshape.305
  129.3 6.7 %copy.65 = bf16[9,2,22,1,8,33]{4,1,5,2,0,3:T(2,128)(2,1)} copy(bf16[9,2,22,1,8,33]{5,4,2,0,1,3:T(8,128)(2,1)S(1)} %reshape.305) | data formatting | bytes 418176 | tf_op jit(solution)/shard_map/conv_general_dilated | solution.py:90
  136.0 1.2 slice.122
  137.3 10.8 %fusion.89 = bf16[9,2,22,8,35]{3,1,4,2,0:T(2,128)(2,1)S(1)} fusion(bf16[9,2,22,1,7,2]{4,1,5,2,0,3:T(2,128)(2,1)S(1)} %slice.122, bf16[9,2,22,1,8,33]{4,1,5,2,0,3:T(2,128)(2,1)} %copy.65), kind=kLoop, calls=%fused_computation.30.clone.clone.1 | loop fusion | flops 665280 | bytes 441936 | tf_op jit(solution)/shard_map/conv_general_dilated | solution.py:90
  148.1 30.3 %fusion.16 = bf16[7,20,1,8,33,32]{5,3,4,1,0,2:T(8,128)(2,1)S(1)} fusion(f32[7,20]{1,0:T(8,128)S(1)} %and_convert_fusion.1, pred[8,33]{0,1:T(8,128)(4,1)S(1)} %copy-done.9, bf16[32,2,3,3,3]{0,1,4,3,2:T(2,128)(2,1)S(1)} %copy-done.7, bf16[9,2,22,8,35]{3,1,4,2,0:T(2,128)(2,1)S(1)} %fusion.89), kind=kOutput, calls=%fused_computation.21 | convolution fusion | flops 133647360 | bytes 2591480 | tf_op jit(solution)/shard_map/conv_general_dilated | solution.py:90
  178.4 0.1 fusion.76
  178.5 0.0 copy-start.8
  178.5 22.8 %fusion.23 = bf16[5,18,1,8,33,32]{5,3,4,1,0,2:T(8,128)(2,1)S(1)} fusion(f32[5,18]{1,0:T(8,128)S(1)} %and_convert_fusion, pred[8,33]{0,1:T(8,128)(4,1)S(1)} %copy-done.9, bf16[32,32,3,3,3]{1,0,4,3,2:T(8,128)(2,1)S(1)} %copy-done, bf16[7,20,1,7,1,32]{5,3,4,1,0,2:T(8,128)(2,1)S(1)} %get-tuple-element.6, ...), kind=kOutput, calls=%fused_computation.27 | convolution fusion | flops 1329418240 | bytes 4067440 | tf_op jit(solution)/shard_map/conv_general_dilated | solution.py:90
  201.3 0.1 fusion.77
  201.4 0.0 copy-start.2
  201.4 0.0 copy-start.4
  201.4 221.1 %fusion.20 = f32[3,16,8,33,2]{2,4,3,1,0:T(2,128)S(1)} fusion(bf16[2,32,3,3,3]{1,0,4,3,2:T(2,128)(2,1)S(1)} %copy-done.8, bf16[5,18,1,7,1,32]{5,3,4,1,0,2:T(8,128)(2,1)S(1)} %get-tuple-element.8, bf16[5,18,1,7,1,32]{5,3,4,1,0,2:T(8,128)(2,1)S(1)} %get-tuple-element.7, bf16[5,18,1,8,33,32]{5,3,4,1,0,2:T(8,128)(2,1)S(1)} %fusion.23), kind=kOutput, calls=%fused_computation.25 | convolution fusion | flops 51858432 | bytes 1706112 | tf_op jit(solution)/shard_map/conv_general_dilated | solution.py:90
  422.5 1.0 copy.77
  423.4 0.2 reshape.304
  423.7 0.6 copy.68
  (19 shorter events, 0.1 us)
Async XLA Ops:
  0.0 178.5 %copy-start = (bf16[32,32,3,3,3]{1,0,4,3,2:T(8,128)(2,1)S(1)}, bf16[32,32,3,3,3]{1,0,4,3,2:T(8,128)(2,1)}, u32[]{:S(2)}) copy-start(bf16[32,32,3,3,3]{1,0,4,3,2:T(8,128)(2,1)} %param.12) | copy-start | bytes 165892
  1.9 19.8 %all-to-all-start = ((bf16[16,3,2,16,256]{4,3,1,2,0:T(8,128)(2,1)}), bf16[16,3,2,16,256]{4,3,1,2,0:T(8,128)(2,1)S(1)}, u32[]{:S(2)}, u32[]{:S(2)}) async-start(bf16[16,3,2,16,256]{4,3,1,2,0:T(8,128)(2,1)} %broadcast_in_dim.4), calls=%async_computation | async-start | bytes 1572864 | tf_op jit(solution)/shard_map/all_to_all | solution.py:11
  22.4 10.9 %copy-start.6 = (s32[256,256]{1,0:T(8,128)S(1)}, s32[256,256]{1,0:T(8,128)}, u32[]{:S(2)}) copy-start(s32[256,256]{1,0:T(8,128)} %param.10) | copy-start | bytes 786436
  24.1 30.9 %all-to-all-start.1 = ((bf16[1,48,2,16,256]{4,3,2,0,1:T(8,128)(2,1)}), bf16[1,48,2,16,256]{4,3,2,0,1:T(8,128)(2,1)S(1)}, u32[]{:S(2)}, u32[]{:S(2)}) async-start(bf16[1,48,2,16,256]{4,3,2,0,1:T(8,128)(2,1)} %maximum_bitcast_fusion), calls=%async_computation.1 | async-start | bytes 1572864 | tf_op jit(solution)/shard_map/all_to_all | solution.py:114
  55.0 1.1 copy-start.5
  84.2 19.8 %copy-start.3 = (f32[3,2,16,256]{3,2,1,0:T(8,128)S(1)}, f32[3,2,16,256]{3,2,1,0:T(8,128)}, u32[]{:S(2)}) copy-start(f32[3,2,16,256]{3,2,1,0:T(8,128)} %param.7) | copy-start | bytes 294916
  85.8 18.0 %all-to-all-start.3 = ((bf16[16,3,2,16,256]{4,3,1,2,0:T(8,128)(2,1)}), bf16[16,3,2,16,256]{4,3,1,2,0:T(8,128)(2,1)S(1)}, u32[]{:S(2)}, u32[]{:S(2)}) async-start(bf16[16,3,2,16,256]{4,3,1,2,0:T(8,128)(2,1)} %copy.60), calls=%async_computation.3 | async-start | bytes 1572864 | tf_op jit(solution)/shard_map/all_to_all | solution.py:34
  103.9 24.5 %copy-start.1 = (f32[3,2,16,256]{3,2,0,1:T(8,128)}, f32[3,2,16,256]{3,2,0,1:T(8,128)S(1)}, u32[]{:S(2)}) copy-start(f32[3,2,16,256]{3,2,0,1:T(8,128)S(1)} %convert_reduce_fusion) | copy-start | bytes 294916
  103.9 7.2 %collective-permute-start.1 = (bf16[3,2,16,256]{3,2,0,1:T(8,128)(2,1)S(1)}, bf16[3,2,16,256]{3,2,0,1:T(8,128)(2,1)S(1)}, u32[]{:S(2)}, u32[]{:S(2)}) collective-permute-start(bf16[3,2,16,256]{3,2,0,1:T(8,128)(2,1)S(1)} %fusion.59), channel_id=1, source_target_pairs={{16,0},{32,16},{48,32},{64,48},{80,64},{96,80},{112,96},{128,112},... | collective-permute-start | bytes 147464 | tf_op jit(solution)/shard_map/ppermute | solution.py:46
  109.2 9.0 %collective-permute-start = (bf16[3,2,16,256]{3,2,0,1:T(8,128)(2,1)S(1)}, bf16[3,2,16,256]{3,2,0,1:T(8,128)(2,1)S(1)}, u32[]{:S(2)}, u32[]{:S(2)}) collective-permute-start(bf16[3,2,16,256]{3,2,0,1:T(8,128)(2,1)S(1)} %fusion.59), channel_id=1, source_target_pairs={{0,16},{16,32},{32,48},{48,64},{64,80},{80,96},{96,112},{112,128},... | collective-permute-start | bytes 147464 | tf_op jit(solution)/shard_map/ppermute | solution.py:45
  118.2 5.8 %collective-permute-start.2 = (bf16[9,2,3,256]{3,2,0,1:T(4,128)(2,1)S(1)}, bf16[9,2,3,256]{3,2,0,1:T(4,128)(2,1)S(1)}, u32[]{:S(2)}, u32[]{:S(2)}) collective-permute-start(bf16[9,2,3,256]{3,2,0,1:T(4,128)(2,1)S(1)} %get-tuple-element.19), channel_id=1, source_target_pairs={{0,1},{1,2},{2,3},{3,4},{4,5},{5,6},{6,7},{7,8},{8,9},{9,10},{10,1... | collective-permute-start | bytes 82952 | tf_op jit(solution)/shard_map/ppermute | solution.py:45
  122.5 5.9 %collective-permute-start.3 = (bf16[9,2,3,256]{3,2,0,1:T(4,128)(2,1)S(1)}, bf16[9,2,3,256]{3,2,0,1:T(4,128)(2,1)S(1)}, u32[]{:S(2)}, u32[]{:S(2)}) collective-permute-start(bf16[9,2,3,256]{3,2,0,1:T(4,128)(2,1)S(1)} %get-tuple-element.20), channel_id=1, source_target_pairs={{1,0},{2,1},{3,2},{4,3},{5,4},{6,5},{7,6},{8,7},{9,8},{10,9},{11,1... | collective-permute-start | bytes 82952 | tf_op jit(solution)/shard_map/ppermute | solution.py:46
  128.6 19.5 %copy-start.7 = (bf16[32,2,3,3,3]{0,1,4,3,2:T(2,128)(2,1)S(1)}, bf16[32,2,3,3,3]{0,1,4,3,2:T(2,128)(2,1)}, u32[]{:S(2)}) copy-start(bf16[32,2,3,3,3]{0,1,4,3,2:T(2,128)(2,1)} %param.11) | copy-start | bytes 10372
  128.6 19.5 %copy-start.9 = (pred[8,33]{0,1:T(8,128)(4,1)S(1)}, pred[8,33]{0,1:T(8,128)(4,1)}, u32[]{:S(2)}) copy-start(pred[8,33]{0,1:T(8,128)(4,1)} %constant.78) | copy-start | bytes 796
  178.5 22.9 %copy-start.8 = (bf16[2,32,3,3,3]{1,0,4,3,2:T(2,128)(2,1)S(1)}, bf16[2,32,3,3,3]{1,0,4,3,2:T(2,128)(2,1)}, u32[]{:S(2)}) copy-start(bf16[2,32,3,3,3]{1,0,4,3,2:T(2,128)(2,1)} %param.13) | copy-start | bytes 10372
  201.4 222.2 %copy-start.2 = (f32[3,2,16,256]{3,2,0,1:T(8,128)S(1)}, f32[3,2,16,256]{3,2,0,1:T(8,128)}, u32[]{:S(2)}) copy-start(f32[3,2,16,256]{3,2,0,1:T(8,128)} %copy-done.1) | copy-start | bytes 294916
  201.4 222.2 %copy-start.4 = (f32[3,2,16,256]{3,2,1,0:T(8,128)S(1)}, f32[3,2,16,256]{3,2,1,0:T(8,128)}, u32[]{:S(2)}) copy-start(f32[3,2,16,256]{3,2,1,0:T(8,128)} %param.7) | copy-start | bytes 294916
where the time goes:
time: 432 us; the launch traced here: 425 us
  matrix products  276 us (64%)
  waiting for transfers between devices  54.3 us (13%)
  starting transfers between devices  34.9 us (8%)
  blocking collectives  25.5 us (6%)
  other arithmetic  18.4 us (4%)
  local copies, waits for them, and re-layouts  14.2 us (3%)
    conv_general_dilated x3, matrix products, convolve(): lax.conv_general_dilated(values[None], weights, (1, 1, 1), ((0, 0), (0, 0...  274 us
    all_to_all x1, blocking collectives, local(): lax.all_to_all(returned, 'slab', split_axis=3, concat_axis=1, tiled=True)  25.5 us
    all_to_all x1, waiting for transfers between devices, local(): lax.all_to_all(lifted, 'slab', split_axis=1, concat_axis=3, tiled=True)  20.7 us
    all_to_all x1, waiting for transfers between devices, summed_on_arrival(): tiles = lax.all_to_all(in_blocks(array, dim, count), axis, 0, 0, tiled=True)  12.2 us
    conv_general_dilated x1, other arithmetic, convolve(): lax.conv_general_dilated(values[None], weights, (1, 1, 1), ((0, 0), (0, 0...  10.8 us
    all_to_all x1, waiting for transfers between devices, sent_to_all(): lax.all_to_all(jnp.broadcast_to(array[None], (count, *array.shape)), axis...  9.84 us
    conv_general_dilated x5, local copies, waits for them, and re-layouts, convolve(): lax.conv_general_dilated(values[None], weights, (1, 1, 1), ((0, 0), (0, 0...  9.76 us
    all_to_all x1, starting transfers between devices, local(): lax.all_to_all(lifted, 'slab', split_axis=1, concat_axis=3, tiled=True)  9.16 us
  transfers between devices with their start and end apart: 7, of which 6 were waited for; matrix products, arithmetic and copies ran while one was open for 1% of the time, Pallas kernels for 0%

commit v1 on v0

v1 whole, which is shorter than its diff:
```python
import math

import jax
import jax.numpy as jnp
import numpy as np
from jax import lax
from jax.experimental import pallas as pl
from jax.experimental.pallas import tpu as pltpu
from jax.sharding import PartitionSpec as P

BF16 = jnp.bfloat16
F32 = jnp.float32
WIN = 24
VMEM = pl.BlockSpec(memory_space=pltpu.VMEM)
SMEM = pl.BlockSpec(memory_space=pltpu.SMEM)


def tables(length):
    ramp = np.arange(length)
    angles = (ramp[:, None] * ramp[None, :] % length) * (2.0 * math.pi / length)
    re = np.cos(angles) / math.sqrt(length)
    im = -np.sin(angles) / math.sqrt(length)
    full = np.block([[re, im], [-im, re]])
    return jnp.asarray(full, BF16), jnp.asarray(full.T, BF16)


def dot(a, b):
    return jnp.dot(a, b, preferred_element_type=F32)


def coil_kernel(place_ref, sens_ref, img_a_ref, img_b_ref, ksp_ref, keep_ref, fwd_ref, bwd_ref,
                keep_out, send_out, pad_ref):
    n = ksp_ref.shape[-1]
    pairs = img_a_ref.shape[0]
    even_here, slot, turn = (place_ref[3] == 0, place_ref[4], place_ref[5])

    def image_part(p):
        planes = []
        for i in range(pairs):
            a, b = (img_a_ref[i ^ slot, 0, p], img_b_ref[i ^ slot, 0, p])
            planes += [jnp.where(even_here, a, b), jnp.where(even_here, b, a)]
        return jnp.concatenate(planes, axis=0).astype(F32)

    sr = sens_ref[:, 0, 0].reshape(n, n).astype(F32)
    si = sens_ref[:, 0, 1].reshape(n, n).astype(F32)
    mr, mi = (image_part(0), image_part(1))
    coil = jnp.concatenate([sr * mr - si * mi, sr * mi + si * mr], axis=1).astype(BF16)
    fwd, bwd = (fwd_ref[...], bwd_ref[...])
    lines = dot(coil, fwd).astype(BF16)
    lines = jnp.concatenate([lines[:, :n], lines[:, n:]], axis=0)
    spectrum = dot(bwd, lines)
    keep = jnp.concatenate([keep_ref[...]] * 2, axis=0).astype(F32)
    misfit = (keep * (spectrum - ksp_ref[0].reshape(2 * n, n).astype(F32))).astype(BF16)
    back = dot(fwd, misfit).astype(BF16)
    back = jnp.concatenate([back[:n], back[n:]], axis=1)
    field = dot(back, bwd)
    fr, fi = (field[:, :n], field[:, n:])
    sr = sens_ref[:, 0, 0].reshape(n, n).astype(F32)
    si = sens_ref[:, 0, 1].reshape(n, n).astype(F32)
    edge = jnp.zeros((8, n), F32)
    for p in range(2):
        pad_ref[p, 0:8] = edge
        pad_ref[p, n + 8 : n + 16] = edge
    pad_ref[0, 8 : n + 8] = sr * fr + si * fi
    pad_ref[1, 8 : n + 8] = sr * fi - si * fr
    depth = n // (2 * pairs)

    def window(j):
        at = j * depth + 4
        return jnp.concatenate([pad_ref[p, at : at + WIN] for p in range(2)], axis=0).astype(BF16)

    for i in range(pairs):
        even, odd = (window(2 * i), window(2 * i + 1))
        keep_out[i ^ turn, 0] = jnp.where(even_here, even, odd)
        send_out[i ^ turn, 0] = jnp.where(even_here, odd, even)


def coil_terms(place, sens, img_a, img_b, ksp, keep, fwd, bwd):
    slabs, rows, parts, depth, n = sens.shape
    pairs = img_a.shape[0]
    out = jax.ShapeDtypeStruct((pairs, rows, 2 * WIN, n), BF16)
    whole = lambda x: (0, 0)
    brick = lambda count: pl.BlockSpec((count, 1, parts, depth, n), lambda x: (0, x, 0, 0, 0))
    out_spec = pl.BlockSpec((pairs, 1, 2 * WIN, n), lambda x: (0, x, 0, 0))
    return pl.pallas_call(
        coil_kernel,
        grid=(rows,),
        in_specs=[
            SMEM,
            brick(slabs),
            brick(pairs),
            brick(pairs),
            pl.BlockSpec((1, parts, n, n), lambda x: (x, 0, 0, 0)),
            pl.BlockSpec((n, n), whole),
            pl.BlockSpec((2 * n, 2 * n), whole),
            pl.BlockSpec((2 * n, 2 * n), whole),
        ],
        out_specs=[out_spec, out_spec],
        out_shape=[out, out],
        scratch_shapes=[pltpu.VMEM((2, n + 16, n), F32)],
        compiler_params=pltpu.CompilerParams(vmem_limit_bytes=40 << 20),
        cost_estimate=pl.CostEstimate(
            flops=rows * 16 * 2 * n * n * n, bytes_accessed=6 << 20, transcendentals=0
        ),
        name="coil_terms",
    )(place, sens, img_a, img_b, ksp, keep, fwd, bwd)


def pair_kernel(a_ref, b_ref, out_ref):
    out_ref[...] = (a_ref[...].astype(F32) + b_ref[...].astype(F32)).astype(BF16)


def pair_sum(a, b):
    return pl.pallas_call(
        pair_kernel,
        in_specs=[VMEM, VMEM],
        out_specs=VMEM,
        out_shape=jax.ShapeDtypeStruct(a.shape, a.dtype),
        compiler_params=pltpu.CompilerParams(vmem_limit_bytes=16 << 20),
        name="pair_sum",
    )(a, b)


def start_kernel(place_ref, terms_ref, img_a_ref, img_b_ref, out_ref):
    pairs, rows = (terms_ref.shape[0], terms_ref.shape[1])
    plane, slot = (place_ref[2], place_ref[4])
    low_pair = jnp.maximum(plane - 1, 0) // 2
    high_pair = jnp.minimum(plane + 1, 2 * pairs - 1) // 2
    low_ok = jnp.where(plane > 0, 1.0, 0.0).astype(F32)
    high_ok = jnp.where(plane < 2 * pairs - 1, 1.0, 0.0).astype(F32)
    depth = img_a_ref.shape[3]
    for x in range(rows):
        total = terms_ref[0, x].astype(F32)
        for k in range(1, pairs):
            total += terms_ref[k, x].astype(F32)
        pieces = []
        for p in range(2):
            low = img_b_ref[low_pair ^ slot, x, p].astype(F32)[depth - 8 :] * low_ok
            own = img_a_ref[0, x, p].astype(F32)
            high = img_b_ref[high_pair ^ slot, x, p].astype(F32)[:8] * high_ok
            pieces.append(jnp.concatenate([low, own, high], axis=0)[4 : 4 + WIN])
        out_ref[x] = (jnp.concatenate(pieces, axis=0) - total).astype(BF16)


def start_brick(place, terms, img_a, img_b):
    _, rows, height, n = terms.shape
    return pl.pallas_call(
        start_kernel,
        in_specs=[SMEM, VMEM, VMEM, VMEM],
        out_specs=VMEM,
        out_shape=jax.ShapeDtypeStruct((rows, height, n), BF16),
        compiler_params=pltpu.CompilerParams(vmem_limit_bytes=16 << 20),
        name="start_brick",
    )(place, terms, img_a, img_b)


def shifted(value, column):
    n = value.shape[1]
    before = jnp.where(column == 0, 0.0, pltpu.roll(value, 1, 1))
    after = jnp.where(column == n - 1, 0.0, pltpu.roll(value, n - 1, 1))
    return before, value, after


def conv_kernel(place_ref, low_ref, own_ref, high_ref, w1_ref, w2_ref, w3_ref, out_ref,
                cols_ref, a1_ref, a2_ref):
    rows, height, n = own_ref.shape
    hid = 32
    ext = 3 * rows
    coil, slab = (place_ref[0], place_ref[1])
    flag = lambda ok: jnp.where(ok, 1.0, 0.0).astype(F32)
    x_low, x_high = (flag(coil > 0), flag(coil < pl.cdiv(48, rows) - 1))
    z_low, z_high = (flag(slab > 0), flag(slab < pl.cdiv(256, 16) - 1))

    for x in range(ext):
        src = (low_ref, own_ref, high_ref)[x // rows]
        value = src[x % rows].astype(F32)
        column = lax.broadcasted_iota(jnp.int32, value.shape, 1)
        for d, part in enumerate(shifted(value, column)):
            at = (x * 3 + d) * height
            cols_ref[at : at + height] = part.astype(BF16)

    column1 = lax.broadcasted_iota(jnp.int32, (w1_ref.shape[0], n), 1)
    w1 = w1_ref[:, : 9 * height]
    for x in range(ext - 2):
        at = x * 3 * height
        value = jnp.maximum(dot(w1, cols_ref[at : at + 9 * height]), 0.0)
        if x < rows - 1:
            value = value * x_low
        if x >= 2 * rows - 1:
            value = value * x_high
        value = jnp.concatenate(
            [value[: 2 * hid] * z_low, value[2 * hid : -2 * hid], value[-2 * hid :] * z_high], axis=0
        )
        for d, part in enumerate(shifted(value, column1)):
            a1_ref[x, d] = part.astype(BF16)

    blocks = 3
    out2 = 6 * hid
    for k in range(blocks):
        parts = {}
        for x in range(ext - 2):
            first = 0 if x <= ext - 5 else x - (ext - 5)
            last = min(x, 2)
            cols = jnp.concatenate([a1_ref[x, d, k * out2 : k * out2 + 256] for d in range(3)], axis=0)
            value = dot(w2_ref[first * out2 : (last + 1) * out2], cols)
            for dx in range(first, last + 1):
                piece = value[(dx - first) * out2 : (dx - first + 1) * out2]
                at = x - dx
                parts[at] = piece if at not in parts else parts[at] + piece
            done = x - 2
            if done >= 0:
                value = jnp.maximum(parts.pop(done), 0.0)
                if done < rows - 2:
                    value = value * x_low
                if done >= 2 * rows - 2:
                    value = value * x_high
                if k == 0:
                    value = jnp.concatenate([value[:hid] * z_low, value[hid:]], axis=0)
                if k == blocks - 1:
                    value = jnp.concatenate([value[:-hid], value[-hid:] * z_high], axis=0)
                a2_ref[done, k * out2 : (k + 1) * out2] = value.astype(BF16)

    depth = 16
    size = 2 * depth
    w3 = w3_ref[:, :576]
    terms = [dot(w3, a2_ref[x]) for x in range(rows + 2)]
    column3 = lax.broadcasted_iota(jnp.int32, (size, n), 1)
    for x in range(rows):
        sums = []
        for d in range(3):
            at = lambda dx: (dx * 3 + d) * size
            sums.append(sum(terms[x + dx][at(dx) : at(dx) + size] for dx in range(3)))
        value = sums[1] + jnp.where(column3 == 0, 0.0, pltpu.roll(sums[0], 1, 1))
        value = value + jnp.where(column3 == n - 1, 0.0, pltpu.roll(sums[2], n - 1, 1))
        half = own_ref[x].astype(F32)
        for p in range(2):
            mine = half[p * WIN + 4 : p * WIN + 4 + depth]
            out_ref[x, p] = mine + value[p * depth : (p + 1) * depth]


def regularized(place, low, own, high, w1, w2, w3, depth):
    rows, height, n = own.shape
    ext = 3 * rows
    return pl.pallas_call(
        conv_kernel,
        in_specs=[SMEM] + [VMEM] * 6,
        out_specs=VMEM,
        out_shape=jax.ShapeDtypeStruct((rows, 2, depth, n), F32),
        scratch_shapes=[
            pltpu.VMEM((ext * 3 * height, n), BF16),
            pltpu.VMEM((ext - 2, 3, 640, n), BF16),
            pltpu.VMEM((ext - 4, 576, n), BF16),
        ],
        compiler_params=pltpu.CompilerParams(vmem_limit_bytes=40 << 20),
        cost_estimate=pl.CostEstimate(flops=6 << 30, bytes_accessed=4 << 20, transcendentals=0),
        name="regularized",
    )(place, low, own, high, w1, w2, w3)


def weights_kernel(b1_ref, b2_ref, b3_ref, keep_ref, fwd_ref, bwd_ref,
                   w1_ref, w2_ref, w3_ref, keep_out, fwd_out, bwd_out):
    keep_out[...] = keep_ref[...].astype(F32).astype(BF16)
    fwd_out[...] = fwd_ref[...]
    bwd_out[...] = bwd_ref[...]
    base = b1_ref[...].astype(F32)
    for a in range(20):
        moved = base if a == 0 else pltpu.roll(base, a, 1)
        w1_ref[a * 32 : (a + 1) * 32] = moved.astype(BF16)
    for dx in range(3):
        for dy in range(3):
            base = b2_ref[dx * 3 + dy].astype(F32)
            for a in range(6):
                moved = base if a == 0 else pltpu.roll(base, a * 32, 1)
                at = (dx * 6 + a) * 32
                w2_ref[at : at + 32, dy * 256 : (dy + 1) * 256] = moved.astype(BF16)
    base = b3_ref[...].astype(F32)
    for t in range(18):
        row = jnp.broadcast_to(base[t : t + 1], (16, base.shape[1]))
        moved = pltpu.roll(row, 0, 1, stride=16, stride_axis=0)
        moved = pltpu.roll(moved, 0, 1, stride=16, stride_axis=0)
        w3_ref[t * 16 : (t + 1) * 16] = moved.astype(BF16)


def banded_weights(conv_in, conv_mid, conv_out, keep, fwd, bwd):
    b1 = jnp.pad(conv_in.transpose(0, 2, 4, 1, 3), ((0, 0),) * 4 + ((1, WIN - 4),))
    b1 = jnp.pad(b1.reshape(32, 18 * WIN), ((0, 0), (0, 512 - 18 * WIN)))
    b2 = conv_mid.transpose(2, 4, 0, 3, 1).reshape(9, 32, 96)
    b2 = jnp.pad(b2, ((0, 0), (0, 0), (0, 160)))
    b3 = conv_out.transpose(2, 4, 0, 3, 1).reshape(18, 96)
    b3 = jnp.pad(b3, ((0, 0), (0, 640 - 96)))
    return pl.pallas_call(
        weights_kernel,
        in_specs=[VMEM] * 6,
        out_specs=[VMEM] * 6,
        out_shape=[
            jax.ShapeDtypeStruct((640, 512), BF16),
            jax.ShapeDtypeStruct((576, 768), BF16),
            jax.ShapeDtypeStruct((288, 640), BF16),
            jax.ShapeDtypeStruct(keep.shape, BF16),
            jax.ShapeDtypeStruct(fwd.shape, BF16),
            jax.ShapeDtypeStruct(bwd.shape, BF16),
        ],
        compiler_params=pltpu.CompilerParams(vmem_limit_bytes=16 << 20),
        name="banded_weights",
    )(b1, b2, b3, keep, fwd, bwd)


def gathered(brick, chips):
    held = brick[None]
    for k in (4, 2, 1):
        came = lax.ppermute(held, "coil", [(i, i ^ (2 * k)) for i in range(2 * chips)])
        held = jnp.stack([held, came], axis=1).reshape(-1, *brick.shape)
    return held


def step(image, sensitivity, kspace, sampling, conv_in, conv_mid, conv_out):
    rows, parts, depth, n = image.shape
    coils, slabs = (lax.axis_size("coil"), lax.axis_size("slab"))
    coil, slab = (lax.axis_index("coil"), lax.axis_index("slab"))
    place = jnp.stack(
        [coil, slab, coil ^ slab, (coil ^ slab) % 2, (coil ^ slab) // 2, slab // 2]
    ).astype(jnp.int32)
    pairs = coils // 2
    chips = [[2 * i + c for i in range(pairs)] for c in range(2)]
    partner = [(i, i ^ 1) for i in range(coils)]
    across = [(a * slabs + b, (a ^ b) * slabs + a) for a in range(coils) for b in range(slabs)]
    w1, w2, w3, keep, fwd, bwd = banded_weights(
        conv_in, conv_mid, conv_out, sampling, *tables(n)
    )

    brick = lax.ppermute(image.astype(BF16), ("coil", "slab"), across)
    sens = lax.all_to_all(
        sensitivity[0].reshape(slabs, rows, parts, depth, n), "slab", 0, 0, tiled=True
    )
    img_a = gathered(brick, pairs)
    img_b = lax.ppermute(img_a, "coil", partner)

    kept, sent = coil_terms(place, sens, img_a, img_b, kspace[0], keep, fwd, bwd)
    terms = pair_sum(kept, lax.ppermute(sent, "coil", partner))
    terms = lax.all_to_all(terms, "coil", 0, 0, tiled=True, axis_index_groups=chips)
    start = start_brick(place, terms, img_a, img_b)

    def to(step):
        return [
            ((a ^ b) * slabs + a, (a + step) * slabs + b)
            for a in range(coils) for b in range(slabs) if 0 <= a + step < coils
        ]

    own = lax.ppermute(start, ("coil", "slab"), to(0))
    low = lax.ppermute(start, ("coil", "slab"), to(1))
    high = lax.ppermute(start, ("coil", "slab"), to(-1))
    return regularized(place, low, own, high, w1, w2, w3, depth)


def solution(mesh):
    return jax.shard_map(
        step,
        mesh=mesh,
        in_specs=(
            P("coil", None, "slab", None),
            P("coil", None, None, "slab", None),
            P("coil", "slab", None, None, None),
            P(),
            P(),
            P(),
            P(),
        ),
        out_specs=P("coil", None, "slab", None),
        check_vma=False,
    )
```

time: 432 us -> 121 us (0.28)
  the two profiles are of different devices: /device:TPU:4 before, /device:TPU:23 now
where the time goes in v1:
time: 121 us; the launch traced here: 120 us
  starting transfers between devices  43.1 us (36%)
  waiting for transfers between devices  35.9 us (30%)
  blocking collectives  14.7 us (12%)
  Pallas kernels  14 us (12%)
  local copies, waits for them, and re-layouts  11.9 us (10%)
    ppermute x1, waiting for transfers between devices, step(): brick = lax.ppermute(image.astype(BF16), ('coil', 'slab'), across)  15.2 us
    all_to_all x1, blocking collectives, step(): lax.all_to_all(terms, 'coil', 0, 0, tiled=True, axis_index_groups=chips)  14.7 us
    unnamed x37, local copies, waits for them, and re-layouts  10.9 us
    ppermute x3, waiting for transfers between devices, gathered(): lax.ppermute(held, 'coil', [(i, i ^ 2 * k) for i in range(2 * chips)])  9.64 us
    all_to_all x1, starting transfers between devices, step(): lax.all_to_all(sensitivity[0].reshape(slabs, rows, parts, depth, n), 'sla...  9.51 us
    pallas_call x1, Pallas kernels, regularized(): pl.pallas_call(conv_kernel, in_specs=[SMEM] + [VMEM] * 6, out_specs=VMEM,...  7.22 us
    ppermute x1, starting transfers between devices, step(): brick = lax.ppermute(image.astype(BF16), ('coil', 'slab'), across)  6.94 us
    ppermute x1, starting transfers between devices, step(): img_b = lax.ppermute(img_a, 'coil', partner)  6.26 us
  transfers between devices with their start and end apart: 10, of which 7 were waited for; matrix products, arithmetic and copies ran while one was open for 1% of the time, Pallas kernels for 1%

profile of v1, /device:TPU:23, one launch (start us, length us, event | category | flops | bytes accessed | tf_op | source)
XLA Modules:
  0.0 120.0 jit_solution(4344139042005773428)
XLA Ops:
  0.0 0.0 copy-start.15
  0.0 9.5 %all-to-all-start = ((bf16[16,3,2,16,256]{4,3,2,1,0:T(8,128)(2,1)}), bf16[16,3,2,16,256]{4,3,2,1,0:T(8,128)(2,1)S(1)}, u32[]{:S(2)}, u32[]{:S(2)}) async-start(bf16[16,3,2,16,256]{4,3,2,1,0:T(8,128)(2,1)} %bitcast.29), calls=%async_computation | async-start | bytes 1572864 | tf_op jit(solution)/shard_map/all_to_all | solution.py:332
  9.5 0.0 copy-done.15
  9.5 6.9 %collective-permute-start = (bf16[3,2,16,256]{3,2,1,0:T(8,128)(2,1)S(1)}, bf16[3,2,16,256]{3,2,1,0:T(8,128)(2,1)S(1)}, u32[]{:S(2)}, u32[]{:S(2)}) collective-permute-start(bf16[3,2,16,256]{3,2,1,0:T(8,128)(2,1)S(1)} %convert_element_type.11), channel_id=1, source_target_pairs={{0,0},{1,16},{2,32},{3,48},{4,64},{5,80},{6,96},{7,112},{8,128},{9... | collective-permute-start | bytes 147464 | tf_op jit(solution)/shard_map/ppermute | solution.py:331
  16.5 15.2 %collective-permute-done = bf16[3,2,16,256]{3,2,1,0:T(8,128)(2,1)S(1)} collective-permute-done((bf16[3,2,16,256]{3,2,1,0:T(8,128)(2,1)S(1)}, bf16[3,2,16,256]{3,2,1,0:T(8,128)(2,1)S(1)}, u32[]{:S(2)}, u32[]{:S(2)}) %collective-permute-start) | collective-permute-done | bytes 49184 | tf_op jit(solution)/shard_map/ppermute | solution.py:331
  31.7 2.9 %collective-permute-start.1 = (bf16[1,3,2,16,256]{4,3,2,1,0:T(8,128)(2,1)S(1)}, bf16[1,3,2,16,256]{4,3,2,1,0:T(8,128)(2,1)S(1)}, u32[]{:S(2)}, u32[]{:S(2)}) collective-permute-start(bf16[1,3,2,16,256]{4,3,2,1,0:T(8,128)(2,1)S(1)} %bitcast.35), channel_id=1, source_target_pairs={{0,128},{16,144},{32,160},{48,176},{64,192},{80,208},{96,224},{112... | collective-permute-start | bytes 147464 | tf_op jit(solution)/shard_map/ppermute | solution.py:311
  34.7 1.5 %collective-permute-done.1 = bf16[1,3,2,16,256]{4,3,2,1,0:T(8,128)(2,1)S(1)} collective-permute-done((bf16[1,3,2,16,256]{4,3,2,1,0:T(8,128)(2,1)S(1)}, bf16[1,3,2,16,256]{4,3,2,1,0:T(8,128)(2,1)S(1)}, u32[]{:S(2)}, u32[]{:S(2)}) %collective-permute-start.1) | collective-permute-done | bytes 49184 | tf_op jit(solution)/shard_map/ppermute | solution.py:311
  36.2 0.1 collective-permute-start.2
  36.3 5.0 %collective-permute-done.2 = bf16[2,3,2,16,256]{4,3,2,1,0:T(8,128)(2,1)S(1)} collective-permute-done((bf16[2,3,2,16,256]{4,3,2,1,0:T(8,128)(2,1)S(1)}, bf16[2,3,2,16,256]{4,3,2,1,0:T(8,128)(2,1)S(1)}, u32[]{:S(2)}, u32[]{:S(2)}) %collective-permute-start.2) | collective-permute-done | bytes 98336 | tf_op jit(solution)/shard_map/ppermute | solution.py:311
  41.3 2.2 %collective-permute-start.3 = (bf16[4,3,2,16,256]{4,3,2,1,0:T(8,128)(2,1)S(1)}, bf16[4,3,2,16,256]{4,3,2,1,0:T(8,128)(2,1)S(1)}, u32[]{:S(2)}, u32[]{:S(2)}) collective-permute-start(bf16[4,3,2,16,256]{4,3,2,1,0:T(8,128)(2,1)S(1)} %bitcast.30), channel_id=1, source_target_pairs={{0,32},{16,48},{32,0},{48,16},{64,96},{80,112},{96,64},{112,80},{1... | collective-permute-start | bytes 589832 | tf_op jit(solution)/shard_map/ppermute | solution.py:311
  43.5 3.2 %collective-permute-done.3 = bf16[4,3,2,16,256]{4,3,2,1,0:T(8,128)(2,1)S(1)} collective-permute-done((bf16[4,3,2,16,256]{4,3,2,1,0:T(8,128)(2,1)S(1)}, bf16[4,3,2,16,256]{4,3,2,1,0:T(8,128)(2,1)S(1)}, u32[]{:S(2)}, u32[]{:S(2)}) %collective-permute-start.3) | collective-permute-done | bytes 196640 | tf_op jit(solution)/shard_map/ppermute | solution.py:311
  46.7 6.3 %collective-permute-start.4 = (bf16[8,3,2,16,256]{4,3,2,1,0:T(8,128)(2,1)S(1)}, bf16[8,3,2,16,256]{4,3,2,1,0:T(8,128)(2,1)S(1)}, u32[]{:S(2)}, u32[]{:S(2)}) collective-permute-start(bf16[8,3,2,16,256]{4,3,2,1,0:T(8,128)(2,1)S(1)} %bitcast.25), channel_id=1, source_target_pairs={{0,16},{16,0},{32,48},{48,32},{64,80},{80,64},{96,112},{112,96},{1... | collective-permute-start | bytes 1179656 | tf_op jit(solution)/shard_map/ppermute | solution.py:336
  53.0 0.0 copy-start.17
  53.0 0.7 copy-done.17
  53.7 0.0 copy-start.16
  53.7 0.1 reshape.23
  53.8 0.6 copy-done.16
  54.4 0.2 copy.18
  54.7 0.0 copy-start.14
  54.7 0.3 pad.16.clone
  55.0 0.0 copy-start.2
  55.0 0.1 reshape.21
  55.1 0.5 copy-done.14
  55.6 0.0 copy-start
  55.6 0.0 copy-start.1
  55.6 0.2 copy.16
  55.8 0.2 reshape.22
  56.0 0.1 stack.45.place_ref
  56.1 0.0 copy-done.2
  56.1 0.6 copy-done
  56.7 0.2 copy-done.1
  56.8 1.3 %banded_weights.1 = (bf16[640,512]{1,0:T(8,128)(2,1)S(1)}, bf16[576,768]{1,0:T(8,128)(2,1)S(1)}, bf16[288,640]{1,0:T(8,128)(2,1)S(1)}, bf16[256,256]{1,0:T(8,128...) custom-call(bf16[32,512]{1,0:T(8,128)(2,1)S(1)} %pad.17.b1_ref, ...), custom_call_target="tpu_custom_call" | custom-call | tf_op jit(solution)/shard_map/banded_weights/pallas_call | solution.py:291
  58.1 0.0 copy-start.3
  58.1 0.9 copy-done.3
  59.0 0.0 copy-start.6
  59.0 0.9 copy-done.6
  59.9 0.0 copy-start.8
  59.9 0.8 copy-done.8
  60.7 0.0 copy-start.10
  60.7 0.8 copy-done.10
  61.5 0.0 copy-start.12
  61.5 0.6 copy-done.12
  62.1 0.0 collective-permute-done.4.img_b_ref
  62.1 0.0 all-to-all-done.sens_ref
  62.1 1.1 copy-done.5
  63.3 1.0 copy-done.9
  64.3 1.0 copy-done.11
  65.4 0.9 copy-done.13
  66.3 4.8 %coil_terms.1 = (bf16[8,3,48,256]{3,2,1,0:T(8,128)(2,1)S(1)}, bf16[8,3,48,256]{3,2,1,0:T(8,128)(2,1)S(1)}) custom-call(s32[6]{0:T(128)S(1)} %stack.45.place_ref, bf16[16,3,2,16,256]{4,3,2,1,0:T(8,128)(2,1)S(1)} %all-to-all-done.sens_ref, bf16[8,3,2,16,256]{4,3,2,1,0:T(8,128)(2,1)S(1)} %bitcast.26, ...), custom_call_target="tpu_custom_call" | custom-call | flops 1610612736 | bytes 6291456 | tf_op jit(solution)/shard_map/coil_terms/pallas_call | solution.py:85
  71.0 0.1 collective-permute-start.5
  71.1 2.0 %collective-permute-done.5.b_ref = bf16[8,3,48,256]{3,2,1,0:T(8,128)(2,1)S(1)} collective-permute-done((bf16[8,3,48,256]{3,2,1,0:T(8,128)(2,1)S(1)}, bf16[8,3,48,256]{3,2,1,0:T(8,128)(2,1)S(1)}, u32[]{:S(2)}, u32[]{:S(2)}) %collective-permute-start.5) | collective-permute-done | bytes 589856 | tf_op jit(solution)/shard_map/ppermute | solution.py:339
  73.1 0.1 pair_sum.1
  73.3 0.0 copy-start.7
  73.3 14.7 %all_to_all.10.terms_ref = bf16[8,3,48,256]{3,2,1,0:T(8,128)(2,1)S(1)} all-to-all(bf16[8,3,48,256]{3,2,1,0:T(8,128)(2,1)S(1)} %pair_sum.1), channel_id=1, replica_groups={{0,32,64,96,128,160,192,224},{16,48,80,112,144,176,208,240},{1,33,65,97..., dimensions={0} | all-to-all | bytes 1179648 | tf_op jit(solution)/shard_map/all_to_all | solution.py:340
  88.0 0.6 start_brick.1
  88.7 6.1 %collective-permute-start.8 = (bf16[3,48,256]{2,1,0:T(8,128)(2,1)S(1)}, bf16[3,48,256]{2,1,0:T(8,128)(2,1)S(1)}, u32[]{:S(2)}, u32[]{:S(2)}) collective-permute-start(bf16[3,48,256]{2,1,0:T(8,128)(2,1)S(1)} %start_brick.1), channel_id=1, source_target_pairs={{17,0},{1,1},{49,2},{33,3},{81,4},{65,5},{113,6},{97,7},{145,8},{1... | collective-permute-start | bytes 221192 | tf_op jit(solution)/shard_map/ppermute | solution.py:351
  94.7 4.5 %collective-permute-start.7 = (bf16[3,48,256]{2,1,0:T(8,128)(2,1)S(1)}, bf16[3,48,256]{2,1,0:T(8,128)(2,1)S(1)}, u32[]{:S(2)}, u32[]{:S(2)}) collective-permute-start(bf16[3,48,256]{2,1,0:T(8,128)(2,1)S(1)} %start_brick.1), channel_id=1, source_target_pairs={{0,0},{16,1},{32,2},{48,3},{64,4},{80,5},{96,6},{112,7},{128,8},{1... | collective-permute-start | bytes 221192 | tf_op jit(solution)/shard_map/ppermute | solution.py:349
  99.3 4.5 %collective-permute-start.6 = (bf16[3,48,256]{2,1,0:T(8,128)(2,1)S(1)}, bf16[3,48,256]{2,1,0:T(8,128)(2,1)S(1)}, u32[]{:S(2)}, u32[]{:S(2)}) collective-permute-start(bf16[3,48,256]{2,1,0:T(8,128)(2,1)S(1)} %start_brick.1), channel_id=1, source_target_pairs={{0,16},{16,17},{32,18},{48,19},{64,20},{80,21},{96,22},{112,23},{1... | collective-permute-start | bytes 221192 | tf_op jit(solution)/shard_map/ppermute | solution.py:350
  103.7 0.0 collective-permute-done.8.high_ref
  103.7 3.5 %collective-permute-done.7.own_ref = bf16[3,48,256]{2,1,0:T(8,128)(2,1)S(1)} collective-permute-done((bf16[3,48,256]{2,1,0:T(8,128)(2,1)S(1)}, bf16[3,48,256]{2,1,0:T(8,128)(2,1)S(1)}, u32[]{:S(2)}, u32[]{:S(2)}) %collective-permute-start.7) | collective-permute-done | bytes 73760 | tf_op jit(solution)/shard_map/ppermute | solution.py:349
  107.3 5.5 %collective-permute-done.6.low_ref = bf16[3,48,256]{2,1,0:T(8,128)(2,1)S(1)} collective-permute-done((bf16[3,48,256]{2,1,0:T(8,128)(2,1)S(1)}, bf16[3,48,256]{2,1,0:T(8,128)(2,1)S(1)}, u32[]{:S(2)}, u32[]{:S(2)}) %collective-permute-start.6) | collective-permute-done | bytes 73760 | tf_op jit(solution)/shard_map/ppermute | solution.py:350
  112.8 0.0 copy-done.7
  112.8 0.0 copy-done.4
  112.8 7.2 %regularized.1 = f32[3,2,16,256]{3,2,1,0:T(8,128)} custom-call(s32[6]{0:T(128)S(1)} %stack.45.place_ref, bf16[3,48,256]{2,1,0:T(8,128)(2,1)S(1)} %collective-permute-done.6.low_ref, bf16[3,48,256]{2,1,0:T(8,128)(2,1)S(1)} %collective-permute-done.7.own_ref, bf16[3,48,256]{2,1,0:T(8,128)(2,1)S(1)} %collective-permute-done.8.high_ref, ...), custom_call_target="tpu_custom_call" | custom-call | flops 6442450944 | bytes 4194304 | tf_op jit(solution)/shard_map/regularized/pallas_call | solution.py:244
  (14 shorter events, 0.2 us)
Async XLA Ops:
  0.0 9.5 %copy-start.15 = (f32[3,2,16,256]{3,2,1,0:T(8,128)S(1)}, f32[3,2,16,256]{3,2,1,0:T(8,128)}, u32[]{:S(2)}) copy-start(f32[3,2,16,256]{3,2,1,0:T(8,128)} %param.9) | copy-start | bytes 294916
  0.0 62.1 %all-to-all-start = ((bf16[16,3,2,16,256]{4,3,2,1,0:T(8,128)(2,1)}), bf16[16,3,2,16,256]{4,3,2,1,0:T(8,128)(2,1)S(1)}, u32[]{:S(2)}, u32[]{:S(2)}) async-start(bf16[16,3,2,16,256]{4,3,2,1,0:T(8,128)(2,1)} %bitcast.29), calls=%async_computation | async-start | bytes 1572864 | tf_op jit(solution)/shard_map/all_to_all | solution.py:332
  9.5 22.2 %collective-permute-start = (bf16[3,2,16,256]{3,2,1,0:T(8,128)(2,1)S(1)}, bf16[3,2,16,256]{3,2,1,0:T(8,128)(2,1)S(1)}, u32[]{:S(2)}, u32[]{:S(2)}) collective-permute-start(bf16[3,2,16,256]{3,2,1,0:T(8,128)(2,1)S(1)} %convert_element_type.11), channel_id=1, source_target_pairs={{0,0},{1,16},{2,32},{3,48},{4,64},{5,80},{6,96},{7,112},{8,128},{9... | collective-permute-start | bytes 147464 | tf_op jit(solution)/shard_map/ppermute | solution.py:331
  31.7 4.4 %collective-permute-start.1 = (bf16[1,3,2,16,256]{4,3,2,1,0:T(8,128)(2,1)S(1)}, bf16[1,3,2,16,256]{4,3,2,1,0:T(8,128)(2,1)S(1)}, u32[]{:S(2)}, u32[]{:S(2)}) collective-permute-start(bf16[1,3,2,16,256]{4,3,2,1,0:T(8,128)(2,1)S(1)} %bitcast.35), channel_id=1, source_target_pairs={{0,128},{16,144},{32,160},{48,176},{64,192},{80,208},{96,224},{112... | collective-permute-start | bytes 147464 | tf_op jit(solution)/shard_map/ppermute | solution.py:311
  36.2 5.1 %collective-permute-start.2 = (bf16[2,3,2,16,256]{4,3,2,1,0:T(8,128)(2,1)S(1)}, bf16[2,3,2,16,256]{4,3,2,1,0:T(8,128)(2,1)S(1)}, u32[]{:S(2)}, u32[]{:S(2)}) collective-permute-start(bf16[2,3,2,16,256]{4,3,2,1,0:T(8,128)(2,1)S(1)} %get-tuple-element.22), channel_id=1, source_target_pairs={{0,64},{16,80},{32,96},{48,112},{64,0},{80,16},{96,32},{112,48},{1... | collective-permute-start | bytes 294920 | tf_op jit(solution)/shard_map/ppermute | solution.py:311
  41.3 5.4 %collective-permute-start.3 = (bf16[4,3,2,16,256]{4,3,2,1,0:T(8,128)(2,1)S(1)}, bf16[4,3,2,16,256]{4,3,2,1,0:T(8,128)(2,1)S(1)}, u32[]{:S(2)}, u32[]{:S(2)}) collective-permute-start(bf16[4,3,2,16,256]{4,3,2,1,0:T(8,128)(2,1)S(1)} %bitcast.30), channel_id=1, source_target_pairs={{0,32},{16,48},{32,0},{48,16},{64,96},{80,112},{96,64},{112,80},{1... | collective-permute-start | bytes 589832 | tf_op jit(solution)/shard_map/ppermute | solution.py:311
  46.7 15.4 %collective-permute-start.4 = (bf16[8,3,2,16,256]{4,3,2,1,0:T(8,128)(2,1)S(1)}, bf16[8,3,2,16,256]{4,3,2,1,0:T(8,128)(2,1)S(1)}, u32[]{:S(2)}, u32[]{:S(2)}) collective-permute-start(bf16[8,3,2,16,256]{4,3,2,1,0:T(8,128)(2,1)S(1)} %bitcast.25), channel_id=1, source_target_pairs={{0,16},{16,0},{32,48},{48,32},{64,80},{80,64},{96,112},{112,96},{1... | collective-permute-start | bytes 1179656 | tf_op jit(solution)/shard_map/ppermute | solution.py:336
  53.0 0.7 copy-start.17
  53.7 0.7 copy-start.16
  54.7 0.9 copy-start.14
  55.0 1.1 copy-start.2
  55.6 1.1 copy-start
  55.6 1.2 %copy-start.1 = (bf16[512,512]{1,0:T(8,128)(2,1)S(1)}, bf16[512,512]{1,0:T(8,128)(2,1)}, u32[]{:S(2)}) copy-start(bf16[512,512]{1,0:T(8,128)(2,1)} %constant.45.clone.fwd_ref) | copy-start | bytes 1572868
  58.1 0.9 copy-start.3
  59.0 0.9 copy-start.6
  59.9 0.8 copy-start.8
  60.7 0.8 copy-start.10
  61.5 0.6 copy-start.12
  62.1 1.1 copy-start.5
  63.3 1.0 copy-start.9
  64.3 1.0 copy-start.11
  65.4 0.9 copy-start.13
  71.0 2.1 %collective-permute-start.5 = (bf16[8,3,48,256]{3,2,1,0:T(8,128)(2,1)S(1)}, bf16[8,3,48,256]{3,2,1,0:T(8,128)(2,1)S(1)}, u32[]{:S(2)}, u32[]{:S(2)}) collective-permute-start(bf16[8,3,48,256]{3,2,1,0:T(8,128)(2,1)S(1)} %get-tuple-element.17), channel_id=1, source_target_pairs={{0,16},{16,0},{32,48},{48,32},{64,80},{80,64},{96,112},{112,96},{1... | collective-permute-start | bytes 1769480 | tf_op jit(solution)/shard_map/ppermute | solution.py:339
  73.3 39.5 %copy-start.7 = (bf16[640,512]{1,0:T(8,128)(2,1)S(1)}, bf16[640,512]{1,0:T(8,128)(2,1)}, u32[]{:S(2)}) copy-start(bf16[640,512]{1,0:T(8,128)(2,1)} %copy-done.6) | copy-start | bytes 1966084
  88.0 24.8 %copy-start.4 = (bf16[576,768]{1,0:T(8,128)(2,1)S(1)}, bf16[576,768]{1,0:T(8,128)(2,1)}, u32[]{:S(2)}) copy-start(bf16[576,768]{1,0:T(8,128)(2,1)} %copy-done.3) | copy-start | bytes 2654212
  88.7 15.1 %collective-permute-start.8 = (bf16[3,48,256]{2,1,0:T(8,128)(2,1)S(1)}, bf16[3,48,256]{2,1,0:T(8,128)(2,1)S(1)}, u32[]{:S(2)}, u32[]{:S(2)}) collective-permute-start(bf16[3,48,256]{2,1,0:T(8,128)(2,1)S(1)} %start_brick.1), channel_id=1, source_target_pairs={{17,0},{1,1},{49,2},{33,3},{81,4},{65,5},{113,6},{97,7},{145,8},{1... | collective-permute-start | bytes 221192 | tf_op jit(solution)/shard_map/ppermute | solution.py:351
  94.7 12.5 %collective-permute-start.7 = (bf16[3,48,256]{2,1,0:T(8,128)(2,1)S(1)}, bf16[3,48,256]{2,1,0:T(8,128)(2,1)S(1)}, u32[]{:S(2)}, u32[]{:S(2)}) collective-permute-start(bf16[3,48,256]{2,1,0:T(8,128)(2,1)S(1)} %start_brick.1), channel_id=1, source_target_pairs={{0,0},{16,1},{32,2},{48,3},{64,4},{80,5},{96,6},{112,7},{128,8},{1... | collective-permute-start | bytes 221192 | tf_op jit(solution)/shard_map/ppermute | solution.py:349
  99.3 13.5 %collective-permute-start.6 = (bf16[3,48,256]{2,1,0:T(8,128)(2,1)S(1)}, bf16[3,48,256]{2,1,0:T(8,128)(2,1)S(1)}, u32[]{:S(2)}, u32[]{:S(2)}) collective-permute-start(bf16[3,48,256]{2,1,0:T(8,128)(2,1)S(1)} %start_brick.1), channel_id=1, source_target_pairs={{0,16},{16,17},{32,18},{48,19},{64,20},{80,21},{96,22},{112,23},{1... | collective-permute-start | bytes 221192 | tf_op jit(solution)/shard_map/ppermute | solution.py:350

commit v2 on v1

--- a/solution.py
+++ b/solution.py
@@ -15,99 +15,105 @@
 SMEM = pl.BlockSpec(memory_space=pltpu.SMEM)
 
 
-def tables(length):
+def table(length):
     ramp = np.arange(length)
     angles = (ramp[:, None] * ramp[None, :] % length) * (2.0 * math.pi / length)
     re = np.cos(angles) / math.sqrt(length)
     im = -np.sin(angles) / math.sqrt(length)
-    full = np.block([[re, im], [-im, re]])
-    return jnp.asarray(full, BF16), jnp.asarray(full.T, BF16)
+    return jnp.asarray(np.concatenate([re, im, -im], axis=1), BF16)
+
+
+def chip_of(z, slab):
+    step = (0x72301456 >> (4 * ((z - slab) & 7))) & 7
+    return ((slab >> 3) ^ (step >> 2)) * 4 + (((slab >> 1) + step) & 3)
+
+
+def plane_of(coil, slab):
+    chip = coil >> 1
+    step = ((chip >> 2) ^ (slab >> 3)) * 4 + ((chip - (slab >> 1)) & 3)
+    return (coil & 1) * 8 + ((slab + ((0x70125634 >> (4 * step)) & 7)) & 7)
+
+
+def coil_of(plane, slab):
+    return 2 * chip_of(plane & 7, slab) + (plane >> 3)
 
 
 def dot(a, b):
     return jnp.dot(a, b, preferred_element_type=F32)
 
 
-def coil_kernel(place_ref, sens_ref, img_a_ref, img_b_ref, ksp_ref, keep_ref, fwd_ref, bwd_ref,
+def coil_kernel(place_ref, sens_ref, img_a_ref, img_b_ref, ksp_ref, keep_ref, table_ref,
                 keep_out, send_out, pad_ref):
-    n = ksp_ref.shape[-1]
-    pairs = img_a_ref.shape[0]
-    even_here, slot, turn = (place_ref[3] == 0, place_ref[4], place_ref[5])
-
-    def image_part(p):
-        planes = []
-        for i in range(pairs):
-            a, b = (img_a_ref[i ^ slot, 0, p], img_b_ref[i ^ slot, 0, p])
-            planes += [jnp.where(even_here, a, b), jnp.where(even_here, b, a)]
-        return jnp.concatenate(planes, axis=0).astype(F32)
-
-    sr = sens_ref[:, 0, 0].reshape(n, n).astype(F32)
-    si = sens_ref[:, 0, 1].reshape(n, n).astype(F32)
-    mr, mi = (image_part(0), image_part(1))
-    coil = jnp.concatenate([sr * mr - si * mi, sr * mi + si * mr], axis=1).astype(BF16)
-    fwd, bwd = (fwd_ref[...], bwd_ref[...])
-    lines = dot(coil, fwd).astype(BF16)
-    lines = jnp.concatenate([lines[:, :n], lines[:, n:]], axis=0)
-    spectrum = dot(bwd, lines)
-    keep = jnp.concatenate([keep_ref[...]] * 2, axis=0).astype(F32)
-    misfit = (keep * (spectrum - ksp_ref[0].reshape(2 * n, n).astype(F32))).astype(BF16)
-    back = dot(fwd, misfit).astype(BF16)
-    back = jnp.concatenate([back[:n], back[n:]], axis=1)
-    field = dot(back, bwd)
-    fr, fi = (field[:, :n], field[:, n:])
-    sr = sens_ref[:, 0, 0].reshape(n, n).astype(F32)
-    si = sens_ref[:, 0, 1].reshape(n, n).astype(F32)
+    rows, n = (ksp_ref.shape[0], ksp_ref.shape[-1])
+    half = img_a_ref.shape[0]
+    coil, slab = (place_ref[0], place_ref[1])
+    chip, low_half = (coil >> 1, (coil & 1) == 0)
+    at = [chip_of(z, slab) for z in range(half)]
+
+    def image_part(x, p):
+        a = jnp.concatenate([img_a_ref[chip ^ at[z], x, p] for z in range(half)], axis=0)
+        b = jnp.concatenate([img_b_ref[chip ^ at[z], x, p] for z in range(half)], axis=0)
+        low, high = (jnp.where(low_half, a, b), jnp.where(low_half, b, a))
+        return jnp.concatenate([low, high], axis=0).astype(F32)
+
+    re, im, mi = (table_ref[:, i * n : (i + 1) * n] for i in range(3))
+    fwd = jnp.concatenate([jnp.concatenate([re, im], axis=1), jnp.concatenate([mi, re], axis=1)], axis=0)
+    bwd = jnp.concatenate([jnp.concatenate([re, mi], axis=1), jnp.concatenate([im, re], axis=1)], axis=0)
+    keep = keep_ref[...].astype(F32)
+    keep = jnp.concatenate([keep, keep], axis=0)
     edge = jnp.zeros((8, n), F32)
-    for p in range(2):
-        pad_ref[p, 0:8] = edge
-        pad_ref[p, n + 8 : n + 16] = edge
-    pad_ref[0, 8 : n + 8] = sr * fr + si * fi
-    pad_ref[1, 8 : n + 8] = sr * fi - si * fr
-    depth = n // (2 * pairs)
-
-    def window(j):
-        at = j * depth + 4
-        return jnp.concatenate([pad_ref[p, at : at + WIN] for p in range(2)], axis=0).astype(BF16)
-
-    for i in range(pairs):
-        even, odd = (window(2 * i), window(2 * i + 1))
-        keep_out[i ^ turn, 0] = jnp.where(even_here, even, odd)
-        send_out[i ^ turn, 0] = jnp.where(even_here, odd, even)
-
-
-def coil_terms(place, sens, img_a, img_b, ksp, keep, fwd, bwd):
-    slabs, rows, parts, depth, n = sens.shape
-    pairs = img_a.shape[0]
-    out = jax.ShapeDtypeStruct((pairs, rows, 2 * WIN, n), BF16)
-    whole = lambda x: (0, 0)
-    brick = lambda count: pl.BlockSpec((count, 1, parts, depth, n), lambda x: (0, x, 0, 0, 0))
-    out_spec = pl.BlockSpec((pairs, 1, 2 * WIN, n), lambda x: (0, x, 0, 0))
+    depth = n // (2 * half)
+    for x in range(rows):
+        sr = sens_ref[:, x, 0].reshape(n, n).astype(F32)
+        si = sens_ref[:, x, 1].reshape(n, n).astype(F32)
+        mr, mi = (image_part(x, 0), image_part(x, 1))
+        coil_image = jnp.concatenate([sr * mr - si * mi, sr * mi + si * mr], axis=1).astype(BF16)
+        lines = dot(coil_image, fwd).astype(BF16)
+        lines = jnp.concatenate([lines[:, :n], lines[:, n:]], axis=0)
+        spectrum = dot(bwd, lines)
+        misfit = (keep * (spectrum - ksp_ref[x].reshape(2 * n, n).astype(F32))).astype(BF16)
+        back = dot(fwd, misfit).astype(BF16)
+        back = jnp.concatenate([back[:n], back[n:]], axis=1)
+        field = dot(back, bwd)
+        fr, fi = (field[:, :n], field[:, n:])
+        sr = sens_ref[:, x, 0].reshape(n, n).astype(F32)
+        si = sens_ref[:, x, 1].reshape(n, n).astype(F32)
+        for p in range(2):
+            pad_ref[x, p, 0:8] = edge
+            pad_ref[x, p, n + 8 : n + 16] = edge
+        pad_ref[x, 0, 8 : n + 8] = sr * fr + si * fi
+        pad_ref[x, 1, 8 : n + 8] = sr * fi - si * fr
+
+        def window(j):
+            first = j * depth + 4
+            parts = [pad_ref[x, p, first : first + WIN] for p in range(2)]
+            return jnp.concatenate(parts, axis=0).astype(BF16)
+
+        for z in range(half):
+            low, high = (window(z), window(half + z))
+            keep_out[at[z], x] = jnp.where(low_half, low, high)
+            send_out[at[z], x] = jnp.where(low_half, high, low)
+
+
+def coil_terms(place, sens, img_a, img_b, ksp, keep, table):
+    _, rows, _, _, n = sens.shape
+    out = jax.ShapeDtypeStruct((img_a.shape[0], rows, 2 * WIN, n), BF16)
     return pl.pallas_call(
         coil_kernel,
-        grid=(rows,),
-        in_specs=[
-            SMEM,
-            brick(slabs),
-            brick(pairs),
-            brick(pairs),
-            pl.BlockSpec((1, parts, n, n), lambda x: (x, 0, 0, 0)),
-            pl.BlockSpec((n, n), whole),
-            pl.BlockSpec((2 * n, 2 * n), whole),
-            pl.BlockSpec((2 * n, 2 * n), whole),
-        ],
-        out_specs=[out_spec, out_spec],
+        in_specs=[SMEM] + [VMEM] * 6,
+        out_specs=[VMEM, VMEM],
         out_shape=[out, out],
-        scratch_shapes=[pltpu.VMEM((2, n + 16, n), F32)],
+        scratch_shapes=[pltpu.VMEM((rows, 2, n + 16, n), F32)],
         compiler_params=pltpu.CompilerParams(vmem_limit_bytes=40 << 20),
         cost_estimate=pl.CostEstimate(
             flops=rows * 16 * 2 * n * n * n, bytes_accessed=6 << 20, transcendentals=0
         ),
         name="coil_terms",
-    )(place, sens, img_a, img_b, ksp, keep, fwd, bwd)
+    )(place, sens, img_a, img_b, ksp, keep, table)
 
 
 def pair_kernel(a_ref, b_ref, out_ref):
-    out_ref[...] = (a_ref[...].astype(F32) + b_ref[...].astype(F32)).astype(BF16)
+    out_ref[...] = a_ref[...] + b_ref[...]
 
 
 def pair_sum(a, b):
@@ -123,11 +129,17 @@
 
 def start_kernel(place_ref, terms_ref, img_a_ref, img_b_ref, out_ref):
     pairs, rows = (terms_ref.shape[0], terms_ref.shape[1])
-    plane, slot = (place_ref[2], place_ref[4])
-    low_pair = jnp.maximum(plane - 1, 0) // 2
-    high_pair = jnp.minimum(plane + 1, 2 * pairs - 1) // 2
+    coil, slab, plane = (place_ref[0], place_ref[1], place_ref[2])
+    chip, half = (coil >> 1, coil & 1)
+    below, above = (jnp.maximum(plane - 1, 0), jnp.minimum(plane + 1, 2 * pairs - 1))
     low_ok = jnp.where(plane > 0, 1.0, 0.0).astype(F32)
     high_ok = jnp.where(plane < 2 * pairs - 1, 1.0, 0.0).astype(F32)
+
+    def brick(j, x, p):
+        slot = chip ^ chip_of(j & 7, slab)
+        value = jnp.where((j >> 3) == half, img_a_ref[slot, x, p], img_b_ref[slot, x, p])
+        return value.astype(F32)
+
     depth = img_a_ref.shape[3]
     for x in range(rows):
         total = terms_ref[0, x].astype(F32)
@@ -135,9 +147,9 @@
             total += terms_ref[k, x].astype(F32)
         pieces = []
         for p in range(2):
-            low = img_b_ref[low_pair ^ slot, x, p].astype(F32)[depth - 8 :] * low_ok
+            low = brick(below, x, p)[depth - 8 :] * low_ok
             own = img_a_ref[0, x, p].astype(F32)
-            high = img_b_ref[high_pair ^ slot, x, p].astype(F32)[:8] * high_ok
+            high = brick(above, x, p)[:8] * high_ok
             pieces.append(jnp.concatenate([low, own, high], axis=0)[4 : 4 + WIN])
         out_ref[x] = (jnp.concatenate(pieces, axis=0) - total).astype(BF16)
 
@@ -257,11 +269,7 @@
     )(place, low, own, high, w1, w2, w3)
 
 
-def weights_kernel(b1_ref, b2_ref, b3_ref, keep_ref, fwd_ref, bwd_ref,
-                   w1_ref, w2_ref, w3_ref, keep_out, fwd_out, bwd_out):
-    keep_out[...] = keep_ref[...].astype(F32).astype(BF16)
-    fwd_out[...] = fwd_ref[...]
-    bwd_out[...] = bwd_ref[...]
+def weights_kernel(b1_ref, b2_ref, b3_ref, w1_ref, w2_ref, w3_ref):
     base = b1_ref[...].astype(F32)
     for a in range(20):
         moved = base if a == 0 else pltpu.roll(base, a, 1)
@@ -281,7 +289,7 @@
         w3_ref[t * 16 : (t + 1) * 16] = moved.astype(BF16)
 
 
-def banded_weights(conv_in, conv_mid, conv_out, keep, fwd, bwd):
+def banded_weights(conv_in, conv_mid, conv_out):
     b1 = jnp.pad(conv_in.transpose(0, 2, 4, 1, 3), ((0, 0),) * 4 + ((1, WIN - 4),))
     b1 = jnp.pad(b1.reshape(32, 18 * WIN), ((0, 0), (0, 512 - 18 * WIN)))
     b2 = conv_mid.transpose(2, 4, 0, 3, 1).reshape(9, 32, 96)
@@ -290,19 +298,16 @@
     b3 = jnp.pad(b3, ((0, 0), (0, 640 - 96)))
     return pl.pallas_call(
         weights_kernel,
-        in_specs=[VMEM] * 6,
-        out_specs=[VMEM] * 6,
+        in_specs=[VMEM] * 3,
+        out_specs=[VMEM] * 3,
         out_shape=[
             jax.ShapeDtypeStruct((640, 512), BF16),
             jax.ShapeDtypeStruct((576, 768), BF16),
             jax.ShapeDtypeStruct((288, 640), BF16),
-            jax.ShapeDtypeStruct(keep.shape, BF16),
-            jax.ShapeDtypeStruct(fwd.shape, BF16),
-            jax.ShapeDtypeStruct(bwd.shape, BF16),
         ],
         compiler_params=pltpu.CompilerParams(vmem_limit_bytes=16 << 20),
         name="banded_weights",
-    )(b1, b2, b3, keep, fwd, bwd)
+    )(b1, b2, b3)
 
 
 def gathered(brick, chips):
@@ -317,16 +322,13 @@
     rows, parts, depth, n = image.shape
     coils, slabs = (lax.axis_size("coil"), lax.axis_size("slab"))
     coil, slab = (lax.axis_index("coil"), lax.axis_index("slab"))
-    place = jnp.stack(
-        [coil, slab, coil ^ slab, (coil ^ slab) % 2, (coil ^ slab) // 2, slab // 2]
-    ).astype(jnp.int32)
+    place = jnp.stack([coil, slab, plane_of(coil, slab)]).astype(jnp.int32)
     pairs = coils // 2
     chips = [[2 * i + c for i in range(pairs)] for c in range(2)]
     partner = [(i, i ^ 1) for i in range(coils)]
-    across = [(a * slabs + b, (a ^ b) * slabs + a) for a in range(coils) for b in range(slabs)]
-    w1, w2, w3, keep, fwd, bwd = banded_weights(
-        conv_in, conv_mid, conv_out, sampling, *tables(n)
-    )
+    there = [(a, b, coil_of(b, a)) for a in range(coils) for b in range(slabs)]
+    across = [(a * slabs + b, c * slabs + a) for a, b, c in there]
+    w1, w2, w3 = banded_weights(conv_in, conv_mid, conv_out)
 
     brick = lax.ppermute(image.astype(BF16), ("coil", "slab"), across)
     sens = lax.all_to_all(
@@ -335,20 +337,16 @@
     img_a = gathered(brick, pairs)
     img_b = lax.ppermute(img_a, "coil", partner)
 
-    kept, sent = coil_terms(place, sens, img_a, img_b, kspace[0], keep, fwd, bwd)
+    kept, sent = coil_terms(place, sens, img_a, img_b, kspace[0], sampling, table(n))
     terms = pair_sum(kept, lax.ppermute(sent, "coil", partner))
     terms = lax.all_to_all(terms, "coil", 0, 0, tiled=True, axis_index_groups=chips)
     start = start_brick(place, terms, img_a, img_b)
 
-    def to(step):
-        return [
-            ((a ^ b) * slabs + a, (a + step) * slabs + b)
-            for a in range(coils) for b in range(slabs) if 0 <= a + step < coils
-        ]
-
-    own = lax.ppermute(start, ("coil", "slab"), to(0))
-    low = lax.ppermute(start, ("coil", "slab"), to(1))
-    high = lax.ppermute(start, ("coil", "slab"), to(-1))
+    home = [(c * slabs + a, a * slabs + b) for a, b, c in there]
+    up = [(i, i + 1) for i in range(coils - 1)]
+    own = lax.ppermute(start, ("coil", "slab"), home)
+    low = lax.ppermute(own, "coil", up)
+    high = lax.ppermute(own, "coil", [(j, i) for i, j in up])
     return regularized(place, low, own, high, w1, w2, w3, depth)
 
 

time: 121 us -> 107 us (0.88)
  the two profiles are of different devices: /device:TPU:23 before, /device:TPU:185 now
where the time goes in v2:
time: 107 us
  waiting for transfers between devices  38.4 us (36%)
  starting transfers between devices  36.1 us (34%)
  blocking collectives  16 us (15%)
  Pallas kernels  13.4 us (13%)
  local copies, waits for them, and re-layouts  2.36 us (2%)
    ppermute x1, waiting for transfers between devices, step(): brick = lax.ppermute(image.astype(BF16), ('coil', 'slab'), across)  17.6 us
    all_to_all x1, blocking collectives, step(): lax.all_to_all(terms, 'coil', 0, 0, tiled=True, axis_index_groups=chips)  16 us
    ppermute x3, starting transfers between devices, gathered(): lax.ppermute(held, 'coil', [(i, i ^ 2 * k) for i in range(2 * chips)])  11.1 us
    ppermute x1, starting transfers between devices, step(): low = lax.ppermute(own, 'coil', up)  9.71 us
    ppermute x3, waiting for transfers between devices, gathered(): lax.ppermute(held, 'coil', [(i, i ^ 2 * k) for i in range(2 * chips)])  7.79 us
    all_to_all x1, starting transfers between devices, step(): lax.all_to_all(sensitivity[0].reshape(slabs, rows, parts, depth, n), 'sla...  7.27 us
    pallas_call x1, Pallas kernels, regularized(): pl.pallas_call(conv_kernel, in_specs=[SMEM] + [VMEM] * 6, out_specs=VMEM,...  7.22 us
    ppermute x1, waiting for transfers between devices, step(): own = lax.ppermute(start, ('coil', 'slab'), home)  6.48 us
  transfers between devices with their start and end apart: 10, of which 8 were waited for; matrix products, arithmetic and copies ran while one was open for 1% of the time, Pallas kernels for 1%

profile of v2, /device:TPU:185, one launch (start us, length us, event | category | flops | bytes accessed | tf_op | source)
XLA Modules:
  0.0 106.6 jit_solution(6784508385441233268)
XLA Ops:
  0.0 0.0 copy-start.4
  0.0 7.3 %all-to-all-start = ((bf16[16,3,2,16,256]{4,3,2,1,0:T(8,128)(2,1)}), bf16[16,3,2,16,256]{4,3,2,1,0:T(8,128)(2,1)S(1)}, u32[]{:S(2)}, u32[]{:S(2)}) async-start(bf16[16,3,2,16,256]{4,3,2,1,0:T(8,128)(2,1)} %bitcast.26), calls=%async_computation | async-start | bytes 1572864 | tf_op jit(solution)/shard_map/all_to_all | solution.py:334
  7.3 0.0 copy-done.4
  7.3 2.2 %collective-permute-start = (bf16[3,2,16,256]{3,2,1,0:T(8,128)(2,1)S(1)}, bf16[3,2,16,256]{3,2,1,0:T(8,128)(2,1)S(1)}, u32[]{:S(2)}, u32[]{:S(2)}) collective-permute-start(bf16[3,2,16,256]{3,2,1,0:T(8,128)(2,1)S(1)} %convert_element_type.11), channel_id=1, source_target_pairs={{0,192},{1,160},{2,128},{3,32},{4,0},{5,96},{6,64},{7,224},{8,208}... | collective-permute-start | bytes 147464 | tf_op jit(solution)/shard_map/ppermute | solution.py:333
  9.5 17.6 %collective-permute-done = bf16[3,2,16,256]{3,2,1,0:T(8,128)(2,1)S(1)} collective-permute-done((bf16[3,2,16,256]{3,2,1,0:T(8,128)(2,1)S(1)}, bf16[3,2,16,256]{3,2,1,0:T(8,128)(2,1)S(1)}, u32[]{:S(2)}, u32[]{:S(2)}) %collective-permute-start) | collective-permute-done | bytes 49184 | tf_op jit(solution)/shard_map/ppermute | solution.py:333
  27.1 3.9 %collective-permute-start.1 = (bf16[1,3,2,16,256]{4,3,2,1,0:T(8,128)(2,1)S(1)}, bf16[1,3,2,16,256]{4,3,2,1,0:T(8,128)(2,1)S(1)}, u32[]{:S(2)}, u32[]{:S(2)}) collective-permute-start(bf16[1,3,2,16,256]{4,3,2,1,0:T(8,128)(2,1)S(1)} %bitcast.32), channel_id=1, source_target_pairs={{0,128},{16,144},{32,160},{48,176},{64,192},{80,208},{96,224},{112... | collective-permute-start | bytes 147464 | tf_op jit(solution)/shard_map/ppermute | solution.py:316
  31.0 1.5 %collective-permute-done.1 = bf16[1,3,2,16,256]{4,3,2,1,0:T(8,128)(2,1)S(1)} collective-permute-done((bf16[1,3,2,16,256]{4,3,2,1,0:T(8,128)(2,1)S(1)}, bf16[1,3,2,16,256]{4,3,2,1,0:T(8,128)(2,1)S(1)}, u32[]{:S(2)}, u32[]{:S(2)}) %collective-permute-start.1) | collective-permute-done | bytes 49184 | tf_op jit(solution)/shard_map/ppermute | solution.py:316
  32.5 3.8 %collective-permute-start.2 = (bf16[2,3,2,16,256]{4,3,2,1,0:T(8,128)(2,1)S(1)}, bf16[2,3,2,16,256]{4,3,2,1,0:T(8,128)(2,1)S(1)}, u32[]{:S(2)}, u32[]{:S(2)}) collective-permute-start(bf16[2,3,2,16,256]{4,3,2,1,0:T(8,128)(2,1)S(1)} %get-tuple-element.16), channel_id=1, source_target_pairs={{0,64},{16,80},{32,96},{48,112},{64,0},{80,16},{96,32},{112,48},{1... | collective-permute-start | bytes 294920 | tf_op jit(solution)/shard_map/ppermute | solution.py:316
  36.2 2.0 %collective-permute-done.2 = bf16[2,3,2,16,256]{4,3,2,1,0:T(8,128)(2,1)S(1)} collective-permute-done((bf16[2,3,2,16,256]{4,3,2,1,0:T(8,128)(2,1)S(1)}, bf16[2,3,2,16,256]{4,3,2,1,0:T(8,128)(2,1)S(1)}, u32[]{:S(2)}, u32[]{:S(2)}) %collective-permute-start.2) | collective-permute-done | bytes 98336 | tf_op jit(solution)/shard_map/ppermute | solution.py:316
  38.3 3.5 %collective-permute-start.3 = (bf16[4,3,2,16,256]{4,3,2,1,0:T(8,128)(2,1)S(1)}, bf16[4,3,2,16,256]{4,3,2,1,0:T(8,128)(2,1)S(1)}, u32[]{:S(2)}, u32[]{:S(2)}) collective-permute-start(bf16[4,3,2,16,256]{4,3,2,1,0:T(8,128)(2,1)S(1)} %bitcast.27), channel_id=1, source_target_pairs={{0,32},{16,48},{32,0},{48,16},{64,96},{80,112},{96,64},{112,80},{1... | collective-permute-start | bytes 589832 | tf_op jit(solution)/shard_map/ppermute | solution.py:316
  41.8 4.3 %collective-permute-done.3 = bf16[4,3,2,16,256]{4,3,2,1,0:T(8,128)(2,1)S(1)} collective-permute-done((bf16[4,3,2,16,256]{4,3,2,1,0:T(8,128)(2,1)S(1)}, bf16[4,3,2,16,256]{4,3,2,1,0:T(8,128)(2,1)S(1)}, u32[]{:S(2)}, u32[]{:S(2)}) %collective-permute-start.3) | collective-permute-done | bytes 196640 | tf_op jit(solution)/shard_map/ppermute | solution.py:316
  46.1 0.0 copy-start
  46.1 0.0 copy-start.1
  46.1 0.0 copy-start.2
  46.2 1.6 %collective-permute-start.4 = (bf16[8,3,2,16,256]{4,3,2,1,0:T(8,128)(2,1)S(1)}, bf16[8,3,2,16,256]{4,3,2,1,0:T(8,128)(2,1)S(1)}, u32[]{:S(2)}, u32[]{:S(2)}) collective-permute-start(bf16[8,3,2,16,256]{4,3,2,1,0:T(8,128)(2,1)S(1)} %bitcast.22), channel_id=1, source_target_pairs={{0,16},{16,0},{32,48},{48,32},{64,80},{80,64},{96,112},{112,96},{1... | collective-permute-start | bytes 1179656 | tf_op jit(solution)/shard_map/ppermute | solution.py:338
  47.8 0.1 pad_add_fusion.place_ref
  47.9 1.3 %collective-permute-done.4.img_b_ref = bf16[8,3,2,16,256]{4,3,2,1,0:T(8,128)(2,1)S(1)} collective-permute-done((bf16[8,3,2,16,256]{4,3,2,1,0:T(8,128)(2,1)S(1)}, bf16[8,3,2,16,256]{4,3,2,1,0:T(8,128)(2,1)S(1)}, u32[]{:S(2)}, u32[]{:S(2)}) %collective-permute-start.4) | collective-permute-done | bytes 393248 | tf_op jit(solution)/shard_map/ppermute | solution.py:338
  49.2 0.0 all-to-all-done.sens_ref
  49.2 0.0 copy-done
  49.2 0.0 copy-done.1
  49.2 0.0 copy-done.2
  49.2 4.2 %coil_terms.1 = (bf16[8,3,48,256]{3,2,1,0:T(8,128)(2,1)S(1)}, bf16[8,3,48,256]{3,2,1,0:T(8,128)(2,1)S(1)}) custom-call(s32[3]{0:T(128)S(1)} %pad_add_fusion.place_ref, bf16[16,3,2,16,256]{4,3,2,1,0:T(8,128)(2,1)S(1)} %all-to-all-done.sens_ref, bf16[8,3,2,16,256]{4,3,2,1,0:T(8,128)(2,1)S(1)} %bitcast.23, ...), custom_call_target="tpu_custom_call" | custom-call | flops 1610612736 | bytes 6291456 | tf_op jit(solution)/shard_map/coil_terms/pallas_call | solution.py:101
  53.4 0.5 collective-permute-start.5
  53.9 1.6 %collective-permute-done.5.b_ref = bf16[8,3,48,256]{3,2,1,0:T(8,128)(2,1)S(1)} collective-permute-done((bf16[8,3,48,256]{3,2,1,0:T(8,128)(2,1)S(1)}, bf16[8,3,48,256]{3,2,1,0:T(8,128)(2,1)S(1)}, u32[]{:S(2)}, u32[]{:S(2)}) %collective-permute-start.5) | collective-permute-done | bytes 589856 | tf_op jit(solution)/shard_map/ppermute | solution.py:341
  55.5 0.1 pair_sum.1
  55.6 16.0 %all_to_all.10.terms_ref = bf16[8,3,48,256]{3,2,1,0:T(8,128)(2,1)S(1)} all-to-all(bf16[8,3,48,256]{3,2,1,0:T(8,128)(2,1)S(1)} %pair_sum.1), channel_id=1, replica_groups={{0,32,64,96,128,160,192,224},{16,48,80,112,144,176,208,240},{1,33,65,97..., dimensions={0} | all-to-all | bytes 1179648 | tf_op jit(solution)/shard_map/all_to_all | solution.py:342
  71.6 0.0 copy-start.3
  71.6 0.6 start_brick.1
  72.3 1.6 %collective-permute-start.6 = (bf16[3,48,256]{2,1,0:T(8,128)(2,1)S(1)}, bf16[3,48,256]{2,1,0:T(8,128)(2,1)S(1)}, u32[]{:S(2)}, u32[]{:S(2)}) collective-permute-start(bf16[3,48,256]{2,1,0:T(8,128)(2,1)S(1)} %start_brick.1), channel_id=1, source_target_pairs={{192,0},{160,1},{128,2},{32,3},{0,4},{96,5},{64,6},{224,7},{208,8}... | collective-permute-start | bytes 221192 | tf_op jit(solution)/shard_map/ppermute | solution.py:347
  73.9 6.5 %collective-permute-done.6.own_ref = bf16[3,48,256]{2,1,0:T(8,128)(2,1)S(1)} collective-permute-done((bf16[3,48,256]{2,1,0:T(8,128)(2,1)S(1)}, bf16[3,48,256]{2,1,0:T(8,128)(2,1)S(1)}, u32[]{:S(2)}, u32[]{:S(2)}) %collective-permute-start.6) | collective-permute-done | bytes 73760 | tf_op jit(solution)/shard_map/ppermute | solution.py:347
  80.4 9.7 %collective-permute-start.7 = (bf16[3,48,256]{2,1,0:T(8,128)(2,1)S(1)}, bf16[3,48,256]{2,1,0:T(8,128)(2,1)S(1)}, u32[]{:S(2)}, u32[]{:S(2)}) collective-permute-start(bf16[3,48,256]{2,1,0:T(8,128)(2,1)S(1)} %collective-permute-done.6.own_ref), channel_id=1, source_target_pairs={{0,16},{16,32},{32,48},{48,64},{64,80},{80,96},{96,112},{112,128},... | collective-permute-start | bytes 221192 | tf_op jit(solution)/shard_map/ppermute | solution.py:348
  90.1 2.1 %collective-permute-start.8 = (bf16[3,48,256]{2,1,0:T(8,128)(2,1)S(1)}, bf16[3,48,256]{2,1,0:T(8,128)(2,1)S(1)}, u32[]{:S(2)}, u32[]{:S(2)}) collective-permute-start(bf16[3,48,256]{2,1,0:T(8,128)(2,1)S(1)} %collective-permute-done.6.own_ref), channel_id=1, source_target_pairs={{16,0},{32,16},{48,32},{64,48},{80,64},{96,80},{112,96},{128,112},... | collective-permute-start | bytes 221192 | tf_op jit(solution)/shard_map/ppermute | solution.py:349
  92.2 0.0 copy-done.3
  92.2 0.2 copy.15
  92.4 0.0 copy-start.5
  92.4 0.2 reshape.22
  92.6 0.5 copy-done.5
  93.1 0.2 copy.17
  93.3 0.3 pad.16.clone
  93.6 0.1 reshape.21
  93.8 0.0 copy-start.6
  93.8 0.7 copy-done.6
  94.5 0.1 reshape.23
  94.6 1.3 %banded_weights.1 = (bf16[640,512]{1,0:T(8,128)(2,1)S(1)}, bf16[576,768]{1,0:T(8,128)(2,1)S(1)}, bf16[288,640]{1,0:T(8,128)(2,1)S(1)}) custom-call(bf16[32,512]{1,0:T(8,128)(2,1)S(1)} %pad.17.b1_ref, bf16[9,32,256]{2,1,0:T(8,128)(2,1)S(1)} %pad.18.b2_ref, bf16[18,640]{1,0:T(8,128)(2,1)S(1)} %pad.19.b3_ref), custom_call_target="tpu_custom_call" | custom-call | tf_op jit(solution)/shard_map/banded_weights/pallas_call | solution.py:299
  95.8 0.0 collective-permute-done.7.low_ref
  95.9 3.5 %collective-permute-done.8.high_ref = bf16[3,48,256]{2,1,0:T(8,128)(2,1)S(1)} collective-permute-done((bf16[3,48,256]{2,1,0:T(8,128)(2,1)S(1)}, bf16[3,48,256]{2,1,0:T(8,128)(2,1)S(1)}, u32[]{:S(2)}, u32[]{:S(2)}) %collective-permute-start.8) | collective-permute-done | bytes 73760 | tf_op jit(solution)/shard_map/ppermute | solution.py:349
  99.4 7.2 %regularized.1 = f32[3,2,16,256]{3,2,1,0:T(8,128)} custom-call(s32[3]{0:T(128)S(1)} %pad_add_fusion.place_ref, bf16[3,48,256]{2,1,0:T(8,128)(2,1)S(1)} %collective-permute-done.7.low_ref, bf16[3,48,256]{2,1,0:T(8,128)(2,1)S(1)} %collective-permute-done.6.own_ref, bf16[3,48,256]{2,1,0:T(8,128)(2,1)S(1)} %collective-permute-done.8.high_ref, ...), custom_call_target="tpu_custom_call" | custom-call | flops 6442450944 | bytes 4194304 | tf_op jit(solution)/shard_map/regularized/pallas_call | solution.py:256
  (9 shorter events, 0.2 us)
Async XLA Ops:
  0.0 7.3 %copy-start.4 = (f32[3,2,16,256]{3,2,1,0:T(8,128)S(1)}, f32[3,2,16,256]{3,2,1,0:T(8,128)}, u32[]{:S(2)}) copy-start(f32[3,2,16,256]{3,2,1,0:T(8,128)} %param.8) | copy-start | bytes 294916
  0.0 49.2 %all-to-all-start = ((bf16[16,3,2,16,256]{4,3,2,1,0:T(8,128)(2,1)}), bf16[16,3,2,16,256]{4,3,2,1,0:T(8,128)(2,1)S(1)}, u32[]{:S(2)}, u32[]{:S(2)}) async-start(bf16[16,3,2,16,256]{4,3,2,1,0:T(8,128)(2,1)} %bitcast.26), calls=%async_computation | async-start | bytes 1572864 | tf_op jit(solution)/shard_map/all_to_all | solution.py:334
  7.3 19.8 %collective-permute-start = (bf16[3,2,16,256]{3,2,1,0:T(8,128)(2,1)S(1)}, bf16[3,2,16,256]{3,2,1,0:T(8,128)(2,1)S(1)}, u32[]{:S(2)}, u32[]{:S(2)}) collective-permute-start(bf16[3,2,16,256]{3,2,1,0:T(8,128)(2,1)S(1)} %convert_element_type.11), channel_id=1, source_target_pairs={{0,192},{1,160},{2,128},{3,32},{4,0},{5,96},{6,64},{7,224},{8,208}... | collective-permute-start | bytes 147464 | tf_op jit(solution)/shard_map/ppermute | solution.py:333
  27.1 5.3 %collective-permute-start.1 = (bf16[1,3,2,16,256]{4,3,2,1,0:T(8,128)(2,1)S(1)}, bf16[1,3,2,16,256]{4,3,2,1,0:T(8,128)(2,1)S(1)}, u32[]{:S(2)}, u32[]{:S(2)}) collective-permute-start(bf16[1,3,2,16,256]{4,3,2,1,0:T(8,128)(2,1)S(1)} %bitcast.32), channel_id=1, source_target_pairs={{0,128},{16,144},{32,160},{48,176},{64,192},{80,208},{96,224},{112... | collective-permute-start | bytes 147464 | tf_op jit(solution)/shard_map/ppermute | solution.py:316
  32.5 5.8 %collective-permute-start.2 = (bf16[2,3,2,16,256]{4,3,2,1,0:T(8,128)(2,1)S(1)}, bf16[2,3,2,16,256]{4,3,2,1,0:T(8,128)(2,1)S(1)}, u32[]{:S(2)}, u32[]{:S(2)}) collective-permute-start(bf16[2,3,2,16,256]{4,3,2,1,0:T(8,128)(2,1)S(1)} %get-tuple-element.16), channel_id=1, source_target_pairs={{0,64},{16,80},{32,96},{48,112},{64,0},{80,16},{96,32},{112,48},{1... | collective-permute-start | bytes 294920 | tf_op jit(solution)/shard_map/ppermute | solution.py:316
  38.3 7.8 %collective-permute-start.3 = (bf16[4,3,2,16,256]{4,3,2,1,0:T(8,128)(2,1)S(1)}, bf16[4,3,2,16,256]{4,3,2,1,0:T(8,128)(2,1)S(1)}, u32[]{:S(2)}, u32[]{:S(2)}) collective-permute-start(bf16[4,3,2,16,256]{4,3,2,1,0:T(8,128)(2,1)S(1)} %bitcast.27), channel_id=1, source_target_pairs={{0,32},{16,48},{32,0},{48,16},{64,96},{80,112},{96,64},{112,80},{1... | collective-permute-start | bytes 589832 | tf_op jit(solution)/shard_map/ppermute | solution.py:316
  46.1 3.1 %copy-start = (bf16[1,3,2,256,256]{4,3,2,1,0:T(8,128)(2,1)S(1)}, bf16[1,3,2,256,256]{4,3,2,1,0:T(8,128)(2,1)}, u32[]{:S(2)}) copy-start(bf16[1,3,2,256,256]{4,3,2,1,0:T(8,128)(2,1)} %param.10) | copy-start | bytes 2359300
  46.1 3.1 %copy-start.1 = (s32[256,256]{1,0:T(8,128)S(1)}, s32[256,256]{1,0:T(8,128)}, u32[]{:S(2)}) copy-start(s32[256,256]{1,0:T(8,128)} %keep_ref.1) | copy-start | bytes 786436
  46.1 3.0 %copy-start.2 = (bf16[256,768]{1,0:T(8,128)(2,1)S(1)}, bf16[256,768]{1,0:T(8,128)(2,1)}, u32[]{:S(2)}) copy-start(bf16[256,768]{1,0:T(8,128)(2,1)} %constant.26.clone.table_ref) | copy-start | bytes 1179652
  46.2 3.0 %collective-permute-start.4 = (bf16[8,3,2,16,256]{4,3,2,1,0:T(8,128)(2,1)S(1)}, bf16[8,3,2,16,256]{4,3,2,1,0:T(8,128)(2,1)S(1)}, u32[]{:S(2)}, u32[]{:S(2)}) collective-permute-start(bf16[8,3,2,16,256]{4,3,2,1,0:T(8,128)(2,1)S(1)} %bitcast.22), channel_id=1, source_target_pairs={{0,16},{16,0},{32,48},{48,32},{64,80},{80,64},{96,112},{112,96},{1... | collective-permute-start | bytes 1179656 | tf_op jit(solution)/shard_map/ppermute | solution.py:338
  53.4 2.1 %collective-permute-start.5 = (bf16[8,3,48,256]{3,2,1,0:T(8,128)(2,1)S(1)}, bf16[8,3,48,256]{3,2,1,0:T(8,128)(2,1)S(1)}, u32[]{:S(2)}, u32[]{:S(2)}) collective-permute-start(bf16[8,3,48,256]{3,2,1,0:T(8,128)(2,1)S(1)} %get-tuple-element.11), channel_id=1, source_target_pairs={{0,16},{16,0},{32,48},{48,32},{64,80},{80,64},{96,112},{112,96},{1... | collective-permute-start | bytes 1769480 | tf_op jit(solution)/shard_map/ppermute | solution.py:341
  71.6 20.6 %copy-start.3 = (bf16[32,32,3,3,3]{1,0,4,3,2:T(8,128)(2,1)S(1)}, bf16[32,32,3,3,3]{1,0,4,3,2:T(8,128)(2,1)}, u32[]{:S(2)}) copy-start(bf16[32,32,3,3,3]{1,0,4,3,2:T(8,128)(2,1)} %param.13) | copy-start | bytes 165892
  72.3 8.1 %collective-permute-start.6 = (bf16[3,48,256]{2,1,0:T(8,128)(2,1)S(1)}, bf16[3,48,256]{2,1,0:T(8,128)(2,1)S(1)}, u32[]{:S(2)}, u32[]{:S(2)}) collective-permute-start(bf16[3,48,256]{2,1,0:T(8,128)(2,1)S(1)} %start_brick.1), channel_id=1, source_target_pairs={{192,0},{160,1},{128,2},{32,3},{0,4},{96,5},{64,6},{224,7},{208,8}... | collective-permute-start | bytes 221192 | tf_op jit(solution)/shard_map/ppermute | solution.py:347
  80.4 15.5 %collective-permute-start.7 = (bf16[3,48,256]{2,1,0:T(8,128)(2,1)S(1)}, bf16[3,48,256]{2,1,0:T(8,128)(2,1)S(1)}, u32[]{:S(2)}, u32[]{:S(2)}) collective-permute-start(bf16[3,48,256]{2,1,0:T(8,128)(2,1)S(1)} %collective-permute-done.6.own_ref), channel_id=1, source_target_pairs={{0,16},{16,32},{32,48},{48,64},{64,80},{80,96},{96,112},{112,128},... | collective-permute-start | bytes 221192 | tf_op jit(solution)/shard_map/ppermute | solution.py:348
  90.1 9.3 %collective-permute-start.8 = (bf16[3,48,256]{2,1,0:T(8,128)(2,1)S(1)}, bf16[3,48,256]{2,1,0:T(8,128)(2,1)S(1)}, u32[]{:S(2)}, u32[]{:S(2)}) collective-permute-start(bf16[3,48,256]{2,1,0:T(8,128)(2,1)S(1)} %collective-permute-done.6.own_ref), channel_id=1, source_target_pairs={{16,0},{32,16},{48,32},{64,48},{80,64},{96,80},{112,96},{128,112},... | collective-permute-start | bytes 221192 | tf_op jit(solution)/shard_map/ppermute | solution.py:349
  92.4 0.7 copy-start.5
  93.8 0.7 copy-start.6

commit v3 on v2

--- a/solution.py
+++ b/solution.py
@@ -23,19 +23,17 @@
     return jnp.asarray(np.concatenate([re, im, -im], axis=1), BF16)
 
 
-def chip_of(z, slab):
-    step = (0x72301456 >> (4 * ((z - slab) & 7))) & 7
-    return ((slab >> 3) ^ (step >> 2)) * 4 + (((slab >> 1) + step) & 3)
-
-
-def plane_of(coil, slab):
+def chip_of(z):
+    return (z & 1) * 4 + (((z >> 1) + 2) & 3)
+
+
+def plane_of(coil):
     chip = coil >> 1
-    step = ((chip >> 2) ^ (slab >> 3)) * 4 + ((chip - (slab >> 1)) & 3)
-    return (coil & 1) * 8 + ((slab + ((0x70125634 >> (4 * step)) & 7)) & 7)
-
-
-def coil_of(plane, slab):
-    return 2 * chip_of(plane & 7, slab) + (plane >> 3)
+    return (coil & 1) * 8 + (((chip - 2) & 3) << 1) + (chip >> 2)
+
+
+def coil_of(plane):
+    return 2 * chip_of(plane & 7) + (plane >> 3)
 
 
 def dot(a, b):
@@ -46,9 +44,9 @@
                 keep_out, send_out, pad_ref):
     rows, n = (ksp_ref.shape[0], ksp_ref.shape[-1])
     half = img_a_ref.shape[0]
-    coil, slab = (place_ref[0], place_ref[1])
+    coil = place_ref[0]
     chip, low_half = (coil >> 1, (coil & 1) == 0)
-    at = [chip_of(z, slab) for z in range(half)]
+    at = [chip_of(z) for z in range(half)]
 
     def image_part(x, p):
         a = jnp.concatenate([img_a_ref[chip ^ at[z], x, p] for z in range(half)], axis=0)
@@ -127,16 +125,16 @@
     )(a, b)
 
 
-def start_kernel(place_ref, terms_ref, img_a_ref, img_b_ref, out_ref):
+def start_kernel(place_ref, terms_ref, img_a_ref, img_b_ref, out_ref, grad_ref):
     pairs, rows = (terms_ref.shape[0], terms_ref.shape[1])
-    coil, slab, plane = (place_ref[0], place_ref[1], place_ref[2])
+    coil, plane = (place_ref[0], place_ref[2])
     chip, half = (coil >> 1, coil & 1)
     below, above = (jnp.maximum(plane - 1, 0), jnp.minimum(plane + 1, 2 * pairs - 1))
     low_ok = jnp.where(plane > 0, 1.0, 0.0).astype(F32)
     high_ok = jnp.where(plane < 2 * pairs - 1, 1.0, 0.0).astype(F32)
 
     def brick(j, x, p):
-        slot = chip ^ chip_of(j & 7, slab)
+        slot = chip ^ chip_of(j & 7)
         value = jnp.where((j >> 3) == half, img_a_ref[slot, x, p], img_b_ref[slot, x, p])
         return value.astype(F32)
 
@@ -152,6 +150,8 @@
             high = brick(above, x, p)[:8] * high_ok
             pieces.append(jnp.concatenate([low, own, high], axis=0)[4 : 4 + WIN])
         out_ref[x] = (jnp.concatenate(pieces, axis=0) - total).astype(BF16)
+        for p in range(2):
+            grad_ref[x, p] = total[p * WIN + 4 : p * WIN + 4 + depth]
 
 
 def start_brick(place, terms, img_a, img_b):
@@ -159,8 +159,11 @@
     return pl.pallas_call(
         start_kernel,
         in_specs=[SMEM, VMEM, VMEM, VMEM],
-        out_specs=VMEM,
-        out_shape=jax.ShapeDtypeStruct((rows, height, n), BF16),
+        out_specs=[VMEM, VMEM],
+        out_shape=[
+            jax.ShapeDtypeStruct((rows, height, n), BF16),
+            jax.ShapeDtypeStruct((rows, *img_a.shape[2:]), F32),
+        ],
         compiler_params=pltpu.CompilerParams(vmem_limit_bytes=16 << 20),
         name="start_brick",
     )(place, terms, img_a, img_b)
@@ -173,15 +176,15 @@
     return before, value, after
 
 
-def conv_kernel(place_ref, low_ref, own_ref, high_ref, w1_ref, w2_ref, w3_ref, out_ref,
+def conv_kernel(place_ref, low_ref, own_ref, high_ref, grad_ref, w1_ref, w2_ref, w3_ref, out_ref,
                 cols_ref, a1_ref, a2_ref):
     rows, height, n = own_ref.shape
     hid = 32
     ext = 3 * rows
-    coil, slab = (place_ref[0], place_ref[1])
+    brick, plane = (place_ref[1], place_ref[2])
     flag = lambda ok: jnp.where(ok, 1.0, 0.0).astype(F32)
-    x_low, x_high = (flag(coil > 0), flag(coil < pl.cdiv(48, rows) - 1))
-    z_low, z_high = (flag(slab > 0), flag(slab < pl.cdiv(256, 16) - 1))
+    x_low, x_high = (flag(brick > 0), flag(brick < 48 // rows - 1))
+    z_low, z_high = (flag(plane > 0), flag(plane < 256 // 16 - 1))
 
     for x in range(ext):
         src = (low_ref, own_ref, high_ref)[x // rows]
@@ -244,20 +247,18 @@
             sums.append(sum(terms[x + dx][at(dx) : at(dx) + size] for dx in range(3)))
         value = sums[1] + jnp.where(column3 == 0, 0.0, pltpu.roll(sums[0], 1, 1))
         value = value + jnp.where(column3 == n - 1, 0.0, pltpu.roll(sums[2], n - 1, 1))
-        half = own_ref[x].astype(F32)
         for p in range(2):
-            mine = half[p * WIN + 4 : p * WIN + 4 + depth]
-            out_ref[x, p] = mine + value[p * depth : (p + 1) * depth]
-
-
-def regularized(place, low, own, high, w1, w2, w3, depth):
+            out_ref[x, p] = (value[p * depth : (p + 1) * depth] - grad_ref[x, p]).astype(BF16)
+
+
+def regularized(place, low, own, high, grad, w1, w2, w3):
     rows, height, n = own.shape
     ext = 3 * rows
     return pl.pallas_call(
         conv_kernel,
-        in_specs=[SMEM] + [VMEM] * 6,
+        in_specs=[SMEM] + [VMEM] * 7,
         out_specs=VMEM,
-        out_shape=jax.ShapeDtypeStruct((rows, 2, depth, n), F32),
+        out_shape=jax.ShapeDtypeStruct(grad.shape, BF16),
         scratch_shapes=[
             pltpu.VMEM((ext * 3 * height, n), BF16),
             pltpu.VMEM((ext - 2, 3, 640, n), BF16),
@@ -266,7 +267,7 @@
         compiler_params=pltpu.CompilerParams(vmem_limit_bytes=40 << 20),
         cost_estimate=pl.CostEstimate(flops=6 << 30, bytes_accessed=4 << 20, transcendentals=0),
         name="regularized",
-    )(place, low, own, high, w1, w2, w3)
+    )(place, low, own, high, grad, w1, w2, w3)
 
 
 def weights_kernel(b1_ref, b2_ref, b3_ref, w1_ref, w2_ref, w3_ref):
@@ -311,22 +312,20 @@
 
 
 def gathered(brick, chips):
-    held = brick[None]
-    for k in (4, 2, 1):
-        came = lax.ppermute(held, "coil", [(i, i ^ (2 * k)) for i in range(2 * chips)])
-        held = jnp.stack([held, came], axis=1).reshape(-1, *brick.shape)
-    return held
+    hop = lambda v, k: lax.ppermute(v, "coil", [(i, i ^ (2 * k)) for i in range(2 * chips)])
+    held = jnp.stack([brick] + [hop(brick, k) for k in (2, 4, 6)])
+    return jnp.stack([held, hop(held, 1)], axis=1).reshape(-1, *brick.shape)
 
 
 def step(image, sensitivity, kspace, sampling, conv_in, conv_mid, conv_out):
     rows, parts, depth, n = image.shape
     coils, slabs = (lax.axis_size("coil"), lax.axis_size("slab"))
     coil, slab = (lax.axis_index("coil"), lax.axis_index("slab"))
-    place = jnp.stack([coil, slab, plane_of(coil, slab)]).astype(jnp.int32)
+    place = jnp.stack([coil, slab, plane_of(coil)]).astype(jnp.int32)
     pairs = coils // 2
     chips = [[2 * i + c for i in range(pairs)] for c in range(2)]
     partner = [(i, i ^ 1) for i in range(coils)]
-    there = [(a, b, coil_of(b, a)) for a in range(coils) for b in range(slabs)]
+    there = [(a, b, coil_of(b)) for a in range(coils) for b in range(slabs)]
     across = [(a * slabs + b, c * slabs + a) for a, b, c in there]
     w1, w2, w3 = banded_weights(conv_in, conv_mid, conv_out)
 
@@ -340,14 +339,16 @@
     kept, sent = coil_terms(place, sens, img_a, img_b, kspace[0], sampling, table(n))
     terms = pair_sum(kept, lax.ppermute(sent, "coil", partner))
     terms = lax.all_to_all(terms, "coil", 0, 0, tiled=True, axis_index_groups=chips)
-    start = start_brick(place, terms, img_a, img_b)
-
-    home = [(c * slabs + a, a * slabs + b) for a, b, c in there]
-    up = [(i, i + 1) for i in range(coils - 1)]
-    own = lax.ppermute(start, ("coil", "slab"), home)
-    low = lax.ppermute(own, "coil", up)
-    high = lax.ppermute(own, "coil", [(j, i) for i, j in up])
-    return regularized(place, low, own, high, w1, w2, w3, depth)
+    start, grad = start_brick(place, terms, img_a, img_b)
+
+    up = [(i, i + 1) for i in range(slabs - 1)]
+    low = lax.ppermute(start, "slab", up)
+    high = lax.ppermute(start, "slab", [(j, i) for i, j in up])
+    change = regularized(place, low, start, high, grad, w1, w2, w3)
+    change = lax.ppermute(
+        change, ("coil", "slab"), [(c * slabs + a, a * slabs + b) for a, b, c in there]
+    )
+    return image + change.astype(F32)
 
 
 def solution(mesh):

time: 107 us -> 105 us (0.981)
  the two profiles are of different devices: /device:TPU:185 before, /device:TPU:4 now
where the time goes in v3:
time: 105 us; the launch traced here: 104 us
  waiting for transfers between devices  38.7 us (37%)
  starting transfers between devices  32.3 us (31%)
  blocking collectives  16.3 us (16%)
  Pallas kernels  12.8 us (12%)
  local copies, waits for them, and re-layouts  2.36 us (2%)
    ppermute x1, waiting for transfers between devices, step(): brick = lax.ppermute(image.astype(BF16), ('coil', 'slab'), across)  18.9 us
    all_to_all x1, blocking collectives, step(): lax.all_to_all(terms, 'coil', 0, 0, tiled=True, axis_index_groups=chips)  16.3 us
    all_to_all x1, starting transfers between devices, step(): lax.all_to_all(sensitivity[0].reshape(slabs, rows, parts, depth, n), 'sla...  9.33 us
    ppermute x4, starting transfers between devices, gathered(): lax.ppermute(v, 'coil', [(i, i ^ 2 * k) for i in range(2 * chips)])  8.94 us
    ppermute x4, waiting for transfers between devices, gathered(): lax.ppermute(v, 'coil', [(i, i ^ 2 * k) for i in range(2 * chips)])  7.87 us
    pallas_call x1, Pallas kernels, regularized(): pl.pallas_call(conv_kernel, in_specs=[SMEM] + [VMEM] * 7, out_specs=VMEM,...  6.56 us
    ppermute x1, starting transfers between devices, step(): lax.ppermute(change, ('coil', 'slab'), [(c * slabs + a, a * slabs + b) fo...  6.24 us
    ppermute x1, waiting for transfers between devices, step(): lax.ppermute(change, ('coil', 'slab'), [(c * slabs + a, a * slabs + b) fo...  5.2 us
  transfers between devices with their start and end apart: 11, of which 7 were waited for; matrix products, arithmetic and copies ran while one was open for 1% of the time, Pallas kernels for 1%

profile of v3, /device:TPU:4, one launch (start us, length us, event | category | flops | bytes accessed | tf_op | source)
XLA Modules:
  0.0 103.5 jit_solution(15682441285905476755)
XLA Ops:
  0.0 0.0 copy-start.3
  0.0 9.3 %all-to-all-start = ((bf16[16,3,2,16,256]{4,3,2,1,0:T(8,128)(2,1)}), bf16[16,3,2,16,256]{4,3,2,1,0:T(8,128)(2,1)S(1)}, u32[]{:S(2)}, u32[]{:S(2)}) async-start(bf16[16,3,2,16,256]{4,3,2,1,0:T(8,128)(2,1)} %bitcast.20), calls=%async_computation | async-start | bytes 1572864 | tf_op jit(solution)/shard_map/all_to_all | solution.py:333
  9.3 0.0 copy-done.3
  9.4 4.0 %collective-permute-start = (bf16[3,2,16,256]{3,2,1,0:T(8,128)(2,1)S(1)}, bf16[3,2,16,256]{3,2,1,0:T(8,128)(2,1)S(1)}, u32[]{:S(2)}, u32[]{:S(2)}) collective-permute-start(bf16[3,2,16,256]{3,2,1,0:T(8,128)(2,1)S(1)} %convert_element_type.14), channel_id=1, source_target_pairs={{0,64},{1,192},{2,96},{3,224},{4,0},{5,128},{6,32},{7,160},{8,80},... | collective-permute-start | bytes 147464 | tf_op jit(solution)/shard_map/ppermute | solution.py:332
  13.3 18.9 %collective-permute-done = bf16[3,2,16,256]{3,2,1,0:T(8,128)(2,1)S(1)} collective-permute-done((bf16[3,2,16,256]{3,2,1,0:T(8,128)(2,1)S(1)}, bf16[3,2,16,256]{3,2,1,0:T(8,128)(2,1)S(1)}, u32[]{:S(2)}, u32[]{:S(2)}) %collective-permute-start) | collective-permute-done | bytes 49184 | tf_op jit(solution)/shard_map/ppermute | solution.py:332
  32.3 0.0 collective-permute-start.1
  32.3 1.4 %collective-permute-start.2 = (bf16[3,2,16,256]{3,2,1,0:T(8,128)(2,1)S(1)}, bf16[3,2,16,256]{3,2,1,0:T(8,128)(2,1)S(1)}, u32[]{:S(2)}, u32[]{:S(2)}) collective-permute-start(bf16[3,2,16,256]{3,2,1,0:T(8,128)(2,1)S(1)} %collective-permute-done), channel_id=1, source_target_pairs={{0,128},{16,144},{32,160},{48,176},{64,192},{80,208},{96,224},{112... | collective-permute-start | bytes 147464 | tf_op jit(solution)/shard_map/ppermute | solution.py:315
  33.7 5.1 %collective-permute-start.3 = (bf16[3,2,16,256]{3,2,1,0:T(8,128)(2,1)S(1)}, bf16[3,2,16,256]{3,2,1,0:T(8,128)(2,1)S(1)}, u32[]{:S(2)}, u32[]{:S(2)}) collective-permute-start(bf16[3,2,16,256]{3,2,1,0:T(8,128)(2,1)S(1)} %collective-permute-done), channel_id=1, source_target_pairs={{0,192},{16,208},{32,224},{48,240},{64,128},{80,144},{96,160},{112... | collective-permute-start | bytes 147464 | tf_op jit(solution)/shard_map/ppermute | solution.py:315
  38.8 0.0 collective-permute-done.1
  38.8 0.0 collective-permute-done.2
  38.8 3.1 %collective-permute-done.3 = bf16[3,2,16,256]{3,2,1,0:T(8,128)(2,1)S(1)} collective-permute-done((bf16[3,2,16,256]{3,2,1,0:T(8,128)(2,1)S(1)}, bf16[3,2,16,256]{3,2,1,0:T(8,128)(2,1)S(1)}, u32[]{:S(2)}, u32[]{:S(2)}) %collective-permute-start.3) | collective-permute-done | bytes 49184 | tf_op jit(solution)/shard_map/ppermute | solution.py:315
  41.9 2.4 %collective-permute-start.4 = (bf16[4,3,2,16,256]{4,3,2,1,0:T(8,128)(2,1)S(1)}, bf16[4,3,2,16,256]{4,3,2,1,0:T(8,128)(2,1)S(1)}, u32[]{:S(2)}, u32[]{:S(2)}) collective-permute-start(bf16[4,3,2,16,256]{4,3,2,1,0:T(8,128)(2,1)S(1)} %get-tuple-element.20), channel_id=1, source_target_pairs={{0,32},{16,48},{32,0},{48,16},{64,96},{80,112},{96,64},{112,80},{1... | collective-permute-start | bytes 589832 | tf_op jit(solution)/shard_map/ppermute | solution.py:315
  44.4 4.8 %collective-permute-done.4 = bf16[4,3,2,16,256]{4,3,2,1,0:T(8,128)(2,1)S(1)} collective-permute-done((bf16[4,3,2,16,256]{4,3,2,1,0:T(8,128)(2,1)S(1)}, bf16[4,3,2,16,256]{4,3,2,1,0:T(8,128)(2,1)S(1)}, u32[]{:S(2)}, u32[]{:S(2)}) %collective-permute-start.4) | collective-permute-done | bytes 196640 | tf_op jit(solution)/shard_map/ppermute | solution.py:315
  49.1 0.0 copy-start
  49.2 0.0 copy-start.1
  49.2 0.0 copy-start.2
  49.2 0.1 collective-permute-start.5
  49.3 0.1 pad_add_fusion.place_ref
  49.4 1.6 %collective-permute-done.5.img_b_ref = bf16[8,3,2,16,256]{4,3,2,1,0:T(8,128)(2,1)S(1)} collective-permute-done((bf16[8,3,2,16,256]{4,3,2,1,0:T(8,128)(2,1)S(1)}, bf16[8,3,2,16,256]{4,3,2,1,0:T(8,128)(2,1)S(1)}, u32[]{:S(2)}, u32[]{:S(2)}) %collective-permute-start.5) | collective-permute-done | bytes 393248 | tf_op jit(solution)/shard_map/ppermute | solution.py:337
  51.0 0.0 all-to-all-done.sens_ref
  51.0 0.0 copy-done
  51.0 0.0 copy-done.1
  51.0 0.0 copy-done.2
  51.0 4.2 %coil_terms.1 = (bf16[8,3,48,256]{3,2,1,0:T(8,128)(2,1)S(1)}, bf16[8,3,48,256]{3,2,1,0:T(8,128)(2,1)S(1)}) custom-call(s32[3]{0:T(128)S(1)} %pad_add_fusion.place_ref, bf16[16,3,2,16,256]{4,3,2,1,0:T(8,128)(2,1)S(1)} %all-to-all-done.sens_ref, bf16[8,3,2,16,256]{4,3,2,1,0:T(8,128)(2,1)S(1)} %bitcast.17, ...), custom_call_target="tpu_custom_call" | custom-call | flops 1610612736 | bytes 6291456 | tf_op jit(solution)/shard_map/coil_terms/pallas_call | solution.py:99
  55.3 0.2 collective-permute-start.6
  55.5 1.9 %collective-permute-done.6.b_ref = bf16[8,3,48,256]{3,2,1,0:T(8,128)(2,1)S(1)} collective-permute-done((bf16[8,3,48,256]{3,2,1,0:T(8,128)(2,1)S(1)}, bf16[8,3,48,256]{3,2,1,0:T(8,128)(2,1)S(1)}, u32[]{:S(2)}, u32[]{:S(2)}) %collective-permute-start.6) | collective-permute-done | bytes 589856 | tf_op jit(solution)/shard_map/ppermute | solution.py:340
  57.4 0.1 pair_sum.1
  57.4 16.3 %all_to_all.10.terms_ref = bf16[8,3,48,256]{3,2,1,0:T(8,128)(2,1)S(1)} all-to-all(bf16[8,3,48,256]{3,2,1,0:T(8,128)(2,1)S(1)} %pair_sum.1), channel_id=1, replica_groups={{0,32,64,96,128,160,192,224},{16,48,80,112,144,176,208,240},{1,33,65,97..., dimensions={0} | all-to-all | bytes 1179648 | tf_op jit(solution)/shard_map/all_to_all | solution.py:341
  73.8 0.0 copy-start.4
  73.8 0.7 start_brick.1
  74.4 2.1 %collective-permute-start.7 = (bf16[3,48,256]{2,1,0:T(8,128)(2,1)S(1)}, bf16[3,48,256]{2,1,0:T(8,128)(2,1)S(1)}, u32[]{:S(2)}, u32[]{:S(2)}) collective-permute-start(bf16[3,48,256]{2,1,0:T(8,128)(2,1)S(1)} %get-tuple-element.14.own_ref), channel_id=1, source_target_pairs={{0,1},{1,2},{2,3},{3,4},{4,5},{5,6},{6,7},{7,8},{8,9},{9,10},{10,1... | collective-permute-start | bytes 221192 | tf_op jit(solution)/shard_map/ppermute | solution.py:345
  76.5 1.5 %collective-permute-start.8 = (bf16[3,48,256]{2,1,0:T(8,128)(2,1)S(1)}, bf16[3,48,256]{2,1,0:T(8,128)(2,1)S(1)}, u32[]{:S(2)}, u32[]{:S(2)}) collective-permute-start(bf16[3,48,256]{2,1,0:T(8,128)(2,1)S(1)} %get-tuple-element.14.own_ref), channel_id=1, source_target_pairs={{1,0},{2,1},{3,2},{4,3},{5,4},{6,5},{7,6},{8,7},{9,8},{10,9},{11,1... | collective-permute-start | bytes 221192 | tf_op jit(solution)/shard_map/ppermute | solution.py:346
  78.0 0.0 copy-done.4
  78.0 0.2 copy.15
  78.1 0.0 copy-start.5
  78.1 0.2 reshape.14
  78.3 0.5 copy-done.5
  78.8 0.2 copy.17
  79.1 0.3 pad.16.clone
  79.4 0.1 reshape.13
  79.5 0.0 copy-start.6
  79.5 0.7 copy-done.6
  80.2 0.1 reshape.15
  80.3 1.3 %banded_weights.1 = (bf16[640,512]{1,0:T(8,128)(2,1)S(1)}, bf16[576,768]{1,0:T(8,128)(2,1)S(1)}, bf16[288,640]{1,0:T(8,128)(2,1)S(1)}) custom-call(bf16[32,512]{1,0:T(8,128)(2,1)S(1)} %pad.17.b1_ref, bf16[9,32,256]{2,1,0:T(8,128)(2,1)S(1)} %pad.18.b2_ref, bf16[18,640]{1,0:T(8,128)(2,1)S(1)} %pad.19.b3_ref), custom_call_target="tpu_custom_call" | custom-call | tf_op jit(solution)/shard_map/banded_weights/pallas_call | solution.py:300
  81.6 0.0 collective-permute-done.7.low_ref
  81.6 3.2 %collective-permute-done.8.high_ref = bf16[3,48,256]{2,1,0:T(8,128)(2,1)S(1)} collective-permute-done((bf16[3,48,256]{2,1,0:T(8,128)(2,1)S(1)}, bf16[3,48,256]{2,1,0:T(8,128)(2,1)S(1)}, u32[]{:S(2)}, u32[]{:S(2)}) %collective-permute-start.8) | collective-permute-done | bytes 73760 | tf_op jit(solution)/shard_map/ppermute | solution.py:346
  84.9 6.6 %regularized.1 = bf16[3,2,16,256]{3,2,1,0:T(8,128)(2,1)S(1)} custom-call(s32[3]{0:T(128)S(1)} %pad_add_fusion.place_ref, bf16[3,48,256]{2,1,0:T(8,128)(2,1)S(1)} %collective-permute-done.7.low_ref, bf16[3,48,256]{2,1,0:T(8,128)(2,1)S(1)} %get-tuple-element.14.own_ref, bf16[3,48,256]{2,1,0:T(8,128)(2,1)S(1)} %collective-permute-done.8.high_ref, ...), custom_call_target="tpu_custom_call" | custom-call | flops 6442450944 | bytes 4194304 | tf_op jit(solution)/shard_map/regularized/pallas_call | solution.py:257
  91.4 6.2 %collective-permute-start.9 = (bf16[3,2,16,256]{3,2,1,0:T(8,128)(2,1)S(1)}, bf16[3,2,16,256]{3,2,1,0:T(8,128)(2,1)S(1)}, u32[]{:S(2)}, u32[]{:S(2)}) collective-permute-start(bf16[3,2,16,256]{3,2,1,0:T(8,128)(2,1)S(1)} %regularized.1), channel_id=1, source_target_pairs={{64,0},{192,1},{96,2},{224,3},{0,4},{128,5},{32,6},{160,7},{80,8},... | collective-permute-start | bytes 147464 | tf_op jit(solution)/shard_map/ppermute | solution.py:348
  97.7 5.2 %collective-permute-done.9 = bf16[3,2,16,256]{3,2,1,0:T(8,128)(2,1)S(1)} collective-permute-done((bf16[3,2,16,256]{3,2,1,0:T(8,128)(2,1)S(1)}, bf16[3,2,16,256]{3,2,1,0:T(8,128)(2,1)S(1)}, u32[]{:S(2)}, u32[]{:S(2)}) %collective-permute-start.9) | collective-permute-done | bytes 49184 | tf_op jit(solution)/shard_map/ppermute | solution.py:348
  102.9 0.7 convert_add_fusion
  (8 shorter events, 0.2 us)
Async XLA Ops:
  0.0 9.3 %copy-start.3 = (f32[3,2,16,256]{3,2,1,0:T(8,128)S(1)}, f32[3,2,16,256]{3,2,1,0:T(8,128)}, u32[]{:S(2)}) copy-start(f32[3,2,16,256]{3,2,1,0:T(8,128)} %param.8) | copy-start | bytes 294916
  0.0 51.0 %all-to-all-start = ((bf16[16,3,2,16,256]{4,3,2,1,0:T(8,128)(2,1)}), bf16[16,3,2,16,256]{4,3,2,1,0:T(8,128)(2,1)S(1)}, u32[]{:S(2)}, u32[]{:S(2)}) async-start(bf16[16,3,2,16,256]{4,3,2,1,0:T(8,128)(2,1)} %bitcast.20), calls=%async_computation | async-start | bytes 1572864 | tf_op jit(solution)/shard_map/all_to_all | solution.py:333
  9.4 22.9 %collective-permute-start = (bf16[3,2,16,256]{3,2,1,0:T(8,128)(2,1)S(1)}, bf16[3,2,16,256]{3,2,1,0:T(8,128)(2,1)S(1)}, u32[]{:S(2)}, u32[]{:S(2)}) collective-permute-start(bf16[3,2,16,256]{3,2,1,0:T(8,128)(2,1)S(1)} %convert_element_type.14), channel_id=1, source_target_pairs={{0,64},{1,192},{2,96},{3,224},{4,0},{5,128},{6,32},{7,160},{8,80},... | collective-permute-start | bytes 147464 | tf_op jit(solution)/shard_map/ppermute | solution.py:332
  32.3 6.5 %collective-permute-start.1 = (bf16[3,2,16,256]{3,2,1,0:T(8,128)(2,1)S(1)}, bf16[3,2,16,256]{3,2,1,0:T(8,128)(2,1)S(1)}, u32[]{:S(2)}, u32[]{:S(2)}) collective-permute-start(bf16[3,2,16,256]{3,2,1,0:T(8,128)(2,1)S(1)} %collective-permute-done), channel_id=1, source_target_pairs={{0,64},{16,80},{32,96},{48,112},{64,0},{80,16},{96,32},{112,48},{1... | collective-permute-start | bytes 147464 | tf_op jit(solution)/shard_map/ppermute | solution.py:315
  32.3 6.5 %collective-permute-start.2 = (bf16[3,2,16,256]{3,2,1,0:T(8,128)(2,1)S(1)}, bf16[3,2,16,256]{3,2,1,0:T(8,128)(2,1)S(1)}, u32[]{:S(2)}, u32[]{:S(2)}) collective-permute-start(bf16[3,2,16,256]{3,2,1,0:T(8,128)(2,1)S(1)} %collective-permute-done), channel_id=1, source_target_pairs={{0,128},{16,144},{32,160},{48,176},{64,192},{80,208},{96,224},{112... | collective-permute-start | bytes 147464 | tf_op jit(solution)/shard_map/ppermute | solution.py:315
  33.7 8.2 %collective-permute-start.3 = (bf16[3,2,16,256]{3,2,1,0:T(8,128)(2,1)S(1)}, bf16[3,2,16,256]{3,2,1,0:T(8,128)(2,1)S(1)}, u32[]{:S(2)}, u32[]{:S(2)}) collective-permute-start(bf16[3,2,16,256]{3,2,1,0:T(8,128)(2,1)S(1)} %collective-permute-done), channel_id=1, source_target_pairs={{0,192},{16,208},{32,224},{48,240},{64,128},{80,144},{96,160},{112... | collective-permute-start | bytes 147464 | tf_op jit(solution)/shard_map/ppermute | solution.py:315
  41.9 7.2 %collective-permute-start.4 = (bf16[4,3,2,16,256]{4,3,2,1,0:T(8,128)(2,1)S(1)}, bf16[4,3,2,16,256]{4,3,2,1,0:T(8,128)(2,1)S(1)}, u32[]{:S(2)}, u32[]{:S(2)}) collective-permute-start(bf16[4,3,2,16,256]{4,3,2,1,0:T(8,128)(2,1)S(1)} %get-tuple-element.20), channel_id=1, source_target_pairs={{0,32},{16,48},{32,0},{48,16},{64,96},{80,112},{96,64},{112,80},{1... | collective-permute-start | bytes 589832 | tf_op jit(solution)/shard_map/ppermute | solution.py:315
  49.1 1.9 %copy-start = (bf16[1,3,2,256,256]{4,3,2,1,0:T(8,128)(2,1)S(1)}, bf16[1,3,2,256,256]{4,3,2,1,0:T(8,128)(2,1)}, u32[]{:S(2)}) copy-start(bf16[1,3,2,256,256]{4,3,2,1,0:T(8,128)(2,1)} %param.10) | copy-start | bytes 2359300
  49.2 1.9 %copy-start.1 = (s32[256,256]{1,0:T(8,128)S(1)}, s32[256,256]{1,0:T(8,128)}, u32[]{:S(2)}) copy-start(s32[256,256]{1,0:T(8,128)} %keep_ref.1) | copy-start | bytes 786436
  49.2 1.9 %copy-start.2 = (bf16[256,768]{1,0:T(8,128)(2,1)S(1)}, bf16[256,768]{1,0:T(8,128)(2,1)}, u32[]{:S(2)}) copy-start(bf16[256,768]{1,0:T(8,128)(2,1)} %constant.22.clone.table_ref) | copy-start | bytes 1179652
  49.2 1.8 %collective-permute-start.5 = (bf16[8,3,2,16,256]{4,3,2,1,0:T(8,128)(2,1)S(1)}, bf16[8,3,2,16,256]{4,3,2,1,0:T(8,128)(2,1)S(1)}, u32[]{:S(2)}, u32[]{:S(2)}) collective-permute-start(bf16[8,3,2,16,256]{4,3,2,1,0:T(8,128)(2,1)S(1)} %bitcast.16), channel_id=1, source_target_pairs={{0,16},{16,0},{32,48},{48,32},{64,80},{80,64},{96,112},{112,96},{1... | collective-permute-start | bytes 1179656 | tf_op jit(solution)/shard_map/ppermute | solution.py:337
  55.3 2.1 %collective-permute-start.6 = (bf16[8,3,48,256]{3,2,1,0:T(8,128)(2,1)S(1)}, bf16[8,3,48,256]{3,2,1,0:T(8,128)(2,1)S(1)}, u32[]{:S(2)}, u32[]{:S(2)}) collective-permute-start(bf16[8,3,48,256]{3,2,1,0:T(8,128)(2,1)S(1)} %get-tuple-element.13), channel_id=1, source_target_pairs={{0,16},{16,0},{32,48},{48,32},{64,80},{80,64},{96,112},{112,96},{1... | collective-permute-start | bytes 1769480 | tf_op jit(solution)/shard_map/ppermute | solution.py:340
  73.8 4.2 %copy-start.4 = (bf16[32,32,3,3,3]{1,0,4,3,2:T(8,128)(2,1)S(1)}, bf16[32,32,3,3,3]{1,0,4,3,2:T(8,128)(2,1)}, u32[]{:S(2)}) copy-start(bf16[32,32,3,3,3]{1,0,4,3,2:T(8,128)(2,1)} %param.13) | copy-start | bytes 165892
  74.4 7.2 %collective-permute-start.7 = (bf16[3,48,256]{2,1,0:T(8,128)(2,1)S(1)}, bf16[3,48,256]{2,1,0:T(8,128)(2,1)S(1)}, u32[]{:S(2)}, u32[]{:S(2)}) collective-permute-start(bf16[3,48,256]{2,1,0:T(8,128)(2,1)S(1)} %get-tuple-element.14.own_ref), channel_id=1, source_target_pairs={{0,1},{1,2},{2,3},{3,4},{4,5},{5,6},{6,7},{7,8},{8,9},{9,10},{10,1... | collective-permute-start | bytes 221192 | tf_op jit(solution)/shard_map/ppermute | solution.py:345
  76.5 8.4 %collective-permute-start.8 = (bf16[3,48,256]{2,1,0:T(8,128)(2,1)S(1)}, bf16[3,48,256]{2,1,0:T(8,128)(2,1)S(1)}, u32[]{:S(2)}, u32[]{:S(2)}) collective-permute-start(bf16[3,48,256]{2,1,0:T(8,128)(2,1)S(1)} %get-tuple-element.14.own_ref), channel_id=1, source_target_pairs={{1,0},{2,1},{3,2},{4,3},{5,4},{6,5},{7,6},{8,7},{9,8},{10,9},{11,1... | collective-permute-start | bytes 221192 | tf_op jit(solution)/shard_map/ppermute | solution.py:346
  78.1 0.7 copy-start.5
  79.5 0.7 copy-start.6
  91.4 11.4 %collective-permute-start.9 = (bf16[3,2,16,256]{3,2,1,0:T(8,128)(2,1)S(1)}, bf16[3,2,16,256]{3,2,1,0:T(8,128)(2,1)S(1)}, u32[]{:S(2)}, u32[]{:S(2)}) collective-permute-start(bf16[3,2,16,256]{3,2,1,0:T(8,128)(2,1)S(1)} %regularized.1), channel_id=1, source_target_pairs={{64,0},{192,1},{96,2},{224,3},{0,4},{128,5},{32,6},{160,7},{80,8},... | collective-permute-start | bytes 147464 | tf_op jit(solution)/shard_map/ppermute | solution.py:348

commit v4 on v3

--- a/solution.py
+++ b/solution.py
@@ -61,18 +61,22 @@
     keep = jnp.concatenate([keep, keep], axis=0)
     edge = jnp.zeros((8, n), F32)
     depth = n // (2 * half)
+    lines, misfits, fields = ([], [], [])
     for x in range(rows):
         sr = sens_ref[:, x, 0].reshape(n, n).astype(F32)
         si = sens_ref[:, x, 1].reshape(n, n).astype(F32)
         mr, mi = (image_part(x, 0), image_part(x, 1))
         coil_image = jnp.concatenate([sr * mr - si * mi, sr * mi + si * mr], axis=1).astype(BF16)
-        lines = dot(coil_image, fwd).astype(BF16)
-        lines = jnp.concatenate([lines[:, :n], lines[:, n:]], axis=0)
-        spectrum = dot(bwd, lines)
-        misfit = (keep * (spectrum - ksp_ref[x].reshape(2 * n, n).astype(F32))).astype(BF16)
-        back = dot(fwd, misfit).astype(BF16)
-        back = jnp.concatenate([back[:n], back[n:]], axis=1)
-        field = dot(back, bwd)
+        lines.append(dot(coil_image, fwd).astype(BF16))
+    for x in range(rows):
+        line = jnp.concatenate([lines[x][:, :n], lines[x][:, n:]], axis=0)
+        spectrum = dot(bwd, line)
+        misfits.append((keep * (spectrum - ksp_ref[x].reshape(2 * n, n).astype(F32))).astype(BF16))
+    for x in range(rows):
+        back = dot(fwd, misfits[x]).astype(BF16)
+        fields.append(jnp.concatenate([back[:n], back[n:]], axis=1))
+    for x in range(rows):
+        field = dot(fields[x], bwd)
         fr, fi = (field[:, :n], field[:, n:])
         sr = sens_ref[:, x, 0].reshape(n, n).astype(F32)
         si = sens_ref[:, x, 1].reshape(n, n).astype(F32)

time: 105 us -> 104 us (level)
  Pallas kernels: 12.8 us -> 11.5 us
    pallas_call x1, Pallas kernels: 4.23 us -> 2.95 us  [coil_terms(): pl.pallas_call(coil_kernel, in_specs=[SMEM] + [VMEM] * 6, out_specs=[VMEM...]
where the time goes in v4:
time: 104 us; the launch traced here: 102 us
  waiting for transfers between devices  38.7 us (37%)
  starting transfers between devices  32.3 us (31%)
  blocking collectives  16.3 us (16%)
  Pallas kernels  11.5 us (11%)
  local copies, waits for them, and re-layouts  2.36 us (2%)
    ppermute x1, waiting for transfers between devices, step(): brick = lax.ppermute(image.astype(BF16), ('coil', 'slab'), across)  18.9 us
    all_to_all x1, blocking collectives, step(): lax.all_to_all(terms, 'coil', 0, 0, tiled=True, axis_index_groups=chips)  16.3 us
    all_to_all x1, starting transfers between devices, step(): lax.all_to_all(sensitivity[0].reshape(slabs, rows, parts, depth, n), 'sla...  9.33 us
    ppermute x4, starting transfers between devices, gathered(): lax.ppermute(v, 'coil', [(i, i ^ 2 * k) for i in range(2 * chips)])  8.94 us
    ppermute x4, waiting for transfers between devices, gathered(): lax.ppermute(v, 'coil', [(i, i ^ 2 * k) for i in range(2 * chips)])  7.87 us
    pallas_call x1, Pallas kernels, regularized(): pl.pallas_call(conv_kernel, in_specs=[SMEM] + [VMEM] * 7, out_specs=VMEM,...  6.55 us
    ppermute x1, starting transfers between devices, step(): lax.ppermute(change, ('coil', 'slab'), [(c * slabs + a, a * slabs + b) fo...  6.25 us
    ppermute x1, waiting for transfers between devices, step(): lax.ppermute(change, ('coil', 'slab'), [(c * slabs + a, a * slabs + b) fo...  5.19 us
  transfers between devices with their start and end apart: 11, of which 7 were waited for; matrix products, arithmetic and copies ran while one was open for 1% of the time, Pallas kernels for 1%

profile of v4, /device:TPU:4, one launch (start us, length us, event | category | flops | bytes accessed | tf_op | source)
XLA Modules:
  0.0 102.2 jit_solution(16449048537740213123)
XLA Ops:
  0.0 0.0 copy-start.3
  0.0 9.3 %all-to-all-start = ((bf16[16,3,2,16,256]{4,3,2,1,0:T(8,128)(2,1)}), bf16[16,3,2,16,256]{4,3,2,1,0:T(8,128)(2,1)S(1)}, u32[]{:S(2)}, u32[]{:S(2)}) async-start(bf16[16,3,2,16,256]{4,3,2,1,0:T(8,128)(2,1)} %bitcast.20), calls=%async_computation | async-start | bytes 1572864 | tf_op jit(solution)/shard_map/all_to_all | solution.py:337
  9.3 0.0 copy-done.3
  9.4 4.0 %collective-permute-start = (bf16[3,2,16,256]{3,2,1,0:T(8,128)(2,1)S(1)}, bf16[3,2,16,256]{3,2,1,0:T(8,128)(2,1)S(1)}, u32[]{:S(2)}, u32[]{:S(2)}) collective-permute-start(bf16[3,2,16,256]{3,2,1,0:T(8,128)(2,1)S(1)} %convert_element_type.14), channel_id=1, source_target_pairs={{0,64},{1,192},{2,96},{3,224},{4,0},{5,128},{6,32},{7,160},{8,80},... | collective-permute-start | bytes 147464 | tf_op jit(solution)/shard_map/ppermute | solution.py:336
  13.3 18.9 %collective-permute-done = bf16[3,2,16,256]{3,2,1,0:T(8,128)(2,1)S(1)} collective-permute-done((bf16[3,2,16,256]{3,2,1,0:T(8,128)(2,1)S(1)}, bf16[3,2,16,256]{3,2,1,0:T(8,128)(2,1)S(1)}, u32[]{:S(2)}, u32[]{:S(2)}) %collective-permute-start) | collective-permute-done | bytes 49184 | tf_op jit(solution)/shard_map/ppermute | solution.py:336
  32.3 0.0 collective-permute-start.1
  32.3 1.4 %collective-permute-start.2 = (bf16[3,2,16,256]{3,2,1,0:T(8,128)(2,1)S(1)}, bf16[3,2,16,256]{3,2,1,0:T(8,128)(2,1)S(1)}, u32[]{:S(2)}, u32[]{:S(2)}) collective-permute-start(bf16[3,2,16,256]{3,2,1,0:T(8,128)(2,1)S(1)} %collective-permute-done), channel_id=1, source_target_pairs={{0,128},{16,144},{32,160},{48,176},{64,192},{80,208},{96,224},{112... | collective-permute-start | bytes 147464 | tf_op jit(solution)/shard_map/ppermute | solution.py:319
  33.7 5.1 %collective-permute-start.3 = (bf16[3,2,16,256]{3,2,1,0:T(8,128)(2,1)S(1)}, bf16[3,2,16,256]{3,2,1,0:T(8,128)(2,1)S(1)}, u32[]{:S(2)}, u32[]{:S(2)}) collective-permute-start(bf16[3,2,16,256]{3,2,1,0:T(8,128)(2,1)S(1)} %collective-permute-done), channel_id=1, source_target_pairs={{0,192},{16,208},{32,224},{48,240},{64,128},{80,144},{96,160},{112... | collective-permute-start | bytes 147464 | tf_op jit(solution)/shard_map/ppermute | solution.py:319
  38.8 0.0 collective-permute-done.1
  38.8 0.0 collective-permute-done.2
  38.8 3.1 %collective-permute-done.3 = bf16[3,2,16,256]{3,2,1,0:T(8,128)(2,1)S(1)} collective-permute-done((bf16[3,2,16,256]{3,2,1,0:T(8,128)(2,1)S(1)}, bf16[3,2,16,256]{3,2,1,0:T(8,128)(2,1)S(1)}, u32[]{:S(2)}, u32[]{:S(2)}) %collective-permute-start.3) | collective-permute-done | bytes 49184 | tf_op jit(solution)/shard_map/ppermute | solution.py:319
  41.9 2.4 %collective-permute-start.4 = (bf16[4,3,2,16,256]{4,3,2,1,0:T(8,128)(2,1)S(1)}, bf16[4,3,2,16,256]{4,3,2,1,0:T(8,128)(2,1)S(1)}, u32[]{:S(2)}, u32[]{:S(2)}) collective-permute-start(bf16[4,3,2,16,256]{4,3,2,1,0:T(8,128)(2,1)S(1)} %get-tuple-element.20), channel_id=1, source_target_pairs={{0,32},{16,48},{32,0},{48,16},{64,96},{80,112},{96,64},{112,80},{1... | collective-permute-start | bytes 589832 | tf_op jit(solution)/shard_map/ppermute | solution.py:319
  44.4 4.8 %collective-permute-done.4 = bf16[4,3,2,16,256]{4,3,2,1,0:T(8,128)(2,1)S(1)} collective-permute-done((bf16[4,3,2,16,256]{4,3,2,1,0:T(8,128)(2,1)S(1)}, bf16[4,3,2,16,256]{4,3,2,1,0:T(8,128)(2,1)S(1)}, u32[]{:S(2)}, u32[]{:S(2)}) %collective-permute-start.4) | collective-permute-done | bytes 196640 | tf_op jit(solution)/shard_map/ppermute | solution.py:319
  49.1 0.0 copy-start
  49.2 0.0 copy-start.1
  49.2 0.0 copy-start.2
  49.2 0.1 collective-permute-start.5
  49.3 0.1 pad_add_fusion.place_ref
  49.4 1.6 %collective-permute-done.5.img_b_ref = bf16[8,3,2,16,256]{4,3,2,1,0:T(8,128)(2,1)S(1)} collective-permute-done((bf16[8,3,2,16,256]{4,3,2,1,0:T(8,128)(2,1)S(1)}, bf16[8,3,2,16,256]{4,3,2,1,0:T(8,128)(2,1)S(1)}, u32[]{:S(2)}, u32[]{:S(2)}) %collective-permute-start.5) | collective-permute-done | bytes 393248 | tf_op jit(solution)/shard_map/ppermute | solution.py:341
  51.0 0.0 all-to-all-done.sens_ref
  51.0 0.0 copy-done
  51.0 0.0 copy-done.1
  51.0 0.0 copy-done.2
  51.0 3.0 %coil_terms.1 = (bf16[8,3,48,256]{3,2,1,0:T(8,128)(2,1)S(1)}, bf16[8,3,48,256]{3,2,1,0:T(8,128)(2,1)S(1)}) custom-call(s32[3]{0:T(128)S(1)} %pad_add_fusion.place_ref, bf16[16,3,2,16,256]{4,3,2,1,0:T(8,128)(2,1)S(1)} %all-to-all-done.sens_ref, bf16[8,3,2,16,256]{4,3,2,1,0:T(8,128)(2,1)S(1)} %bitcast.17, ...), custom_call_target="tpu_custom_call" | custom-call | flops 1610612736 | bytes 6291456 | tf_op jit(solution)/shard_map/coil_terms/pallas_call | solution.py:103
  54.0 0.2 collective-permute-start.6
  54.2 1.9 %collective-permute-done.6.b_ref = bf16[8,3,48,256]{3,2,1,0:T(8,128)(2,1)S(1)} collective-permute-done((bf16[8,3,48,256]{3,2,1,0:T(8,128)(2,1)S(1)}, bf16[8,3,48,256]{3,2,1,0:T(8,128)(2,1)S(1)}, u32[]{:S(2)}, u32[]{:S(2)}) %collective-permute-start.6) | collective-permute-done | bytes 589856 | tf_op jit(solution)/shard_map/ppermute | solution.py:344
  56.1 0.1 pair_sum.1
  56.2 16.3 %all_to_all.10.terms_ref = bf16[8,3,48,256]{3,2,1,0:T(8,128)(2,1)S(1)} all-to-all(bf16[8,3,48,256]{3,2,1,0:T(8,128)(2,1)S(1)} %pair_sum.1), channel_id=1, replica_groups={{0,32,64,96,128,160,192,224},{16,48,80,112,144,176,208,240},{1,33,65,97..., dimensions={0} | all-to-all | bytes 1179648 | tf_op jit(solution)/shard_map/all_to_all | solution.py:345
  72.5 0.0 copy-start.4
  72.5 0.7 start_brick.1
  73.1 2.1 %collective-permute-start.7 = (bf16[3,48,256]{2,1,0:T(8,128)(2,1)S(1)}, bf16[3,48,256]{2,1,0:T(8,128)(2,1)S(1)}, u32[]{:S(2)}, u32[]{:S(2)}) collective-permute-start(bf16[3,48,256]{2,1,0:T(8,128)(2,1)S(1)} %get-tuple-element.14.own_ref), channel_id=1, source_target_pairs={{0,1},{1,2},{2,3},{3,4},{4,5},{5,6},{6,7},{7,8},{8,9},{9,10},{10,1... | collective-permute-start | bytes 221192 | tf_op jit(solution)/shard_map/ppermute | solution.py:349
  75.2 1.5 %collective-permute-start.8 = (bf16[3,48,256]{2,1,0:T(8,128)(2,1)S(1)}, bf16[3,48,256]{2,1,0:T(8,128)(2,1)S(1)}, u32[]{:S(2)}, u32[]{:S(2)}) collective-permute-start(bf16[3,48,256]{2,1,0:T(8,128)(2,1)S(1)} %get-tuple-element.14.own_ref), channel_id=1, source_target_pairs={{1,0},{2,1},{3,2},{4,3},{5,4},{6,5},{7,6},{8,7},{9,8},{10,9},{11,1... | collective-permute-start | bytes 221192 | tf_op jit(solution)/shard_map/ppermute | solution.py:350
  76.7 0.0 copy-done.4
  76.7 0.2 copy.15
  76.9 0.0 copy-start.5
  76.9 0.2 reshape.14
  77.0 0.5 copy-done.5
  77.6 0.2 copy.17
  77.8 0.3 pad.16.clone
  78.1 0.1 reshape.13
  78.3 0.0 copy-start.6
  78.3 0.7 copy-done.6
  79.0 0.1 reshape.15
  79.1 1.3 %banded_weights.1 = (bf16[640,512]{1,0:T(8,128)(2,1)S(1)}, bf16[576,768]{1,0:T(8,128)(2,1)S(1)}, bf16[288,640]{1,0:T(8,128)(2,1)S(1)}) custom-call(bf16[32,512]{1,0:T(8,128)(2,1)S(1)} %pad.17.b1_ref, bf16[9,32,256]{2,1,0:T(8,128)(2,1)S(1)} %pad.18.b2_ref, bf16[18,640]{1,0:T(8,128)(2,1)S(1)} %pad.19.b3_ref), custom_call_target="tpu_custom_call" | custom-call | tf_op jit(solution)/shard_map/banded_weights/pallas_call | solution.py:304
  80.3 0.0 collective-permute-done.7.low_ref
  80.4 3.2 %collective-permute-done.8.high_ref = bf16[3,48,256]{2,1,0:T(8,128)(2,1)S(1)} collective-permute-done((bf16[3,48,256]{2,1,0:T(8,128)(2,1)S(1)}, bf16[3,48,256]{2,1,0:T(8,128)(2,1)S(1)}, u32[]{:S(2)}, u32[]{:S(2)}) %collective-permute-start.8) | collective-permute-done | bytes 73760 | tf_op jit(solution)/shard_map/ppermute | solution.py:350
  83.6 6.6 %regularized.1 = bf16[3,2,16,256]{3,2,1,0:T(8,128)(2,1)S(1)} custom-call(s32[3]{0:T(128)S(1)} %pad_add_fusion.place_ref, bf16[3,48,256]{2,1,0:T(8,128)(2,1)S(1)} %collective-permute-done.7.low_ref, bf16[3,48,256]{2,1,0:T(8,128)(2,1)S(1)} %get-tuple-element.14.own_ref, bf16[3,48,256]{2,1,0:T(8,128)(2,1)S(1)} %collective-permute-done.8.high_ref, ...), custom_call_target="tpu_custom_call" | custom-call | flops 6442450944 | bytes 4194304 | tf_op jit(solution)/shard_map/regularized/pallas_call | solution.py:261
  90.1 6.2 %collective-permute-start.9 = (bf16[3,2,16,256]{3,2,1,0:T(8,128)(2,1)S(1)}, bf16[3,2,16,256]{3,2,1,0:T(8,128)(2,1)S(1)}, u32[]{:S(2)}, u32[]{:S(2)}) collective-permute-start(bf16[3,2,16,256]{3,2,1,0:T(8,128)(2,1)S(1)} %regularized.1), channel_id=1, source_target_pairs={{64,0},{192,1},{96,2},{224,3},{0,4},{128,5},{32,6},{160,7},{80,8},... | collective-permute-start | bytes 147464 | tf_op jit(solution)/shard_map/ppermute | solution.py:352
  96.4 5.2 %collective-permute-done.9 = bf16[3,2,16,256]{3,2,1,0:T(8,128)(2,1)S(1)} collective-permute-done((bf16[3,2,16,256]{3,2,1,0:T(8,128)(2,1)S(1)}, bf16[3,2,16,256]{3,2,1,0:T(8,128)(2,1)S(1)}, u32[]{:S(2)}, u32[]{:S(2)}) %collective-permute-start.9) | collective-permute-done | bytes 49184 | tf_op jit(solution)/shard_map/ppermute | solution.py:352
  101.6 0.7 convert_add_fusion
  (8 shorter events, 0.2 us)
Async XLA Ops:
  0.0 9.3 %copy-start.3 = (f32[3,2,16,256]{3,2,1,0:T(8,128)S(1)}, f32[3,2,16,256]{3,2,1,0:T(8,128)}, u32[]{:S(2)}) copy-start(f32[3,2,16,256]{3,2,1,0:T(8,128)} %param.8) | copy-start | bytes 294916
  0.0 51.0 %all-to-all-start = ((bf16[16,3,2,16,256]{4,3,2,1,0:T(8,128)(2,1)}), bf16[16,3,2,16,256]{4,3,2,1,0:T(8,128)(2,1)S(1)}, u32[]{:S(2)}, u32[]{:S(2)}) async-start(bf16[16,3,2,16,256]{4,3,2,1,0:T(8,128)(2,1)} %bitcast.20), calls=%async_computation | async-start | bytes 1572864 | tf_op jit(solution)/shard_map/all_to_all | solution.py:337
  9.4 22.9 %collective-permute-start = (bf16[3,2,16,256]{3,2,1,0:T(8,128)(2,1)S(1)}, bf16[3,2,16,256]{3,2,1,0:T(8,128)(2,1)S(1)}, u32[]{:S(2)}, u32[]{:S(2)}) collective-permute-start(bf16[3,2,16,256]{3,2,1,0:T(8,128)(2,1)S(1)} %convert_element_type.14), channel_id=1, source_target_pairs={{0,64},{1,192},{2,96},{3,224},{4,0},{5,128},{6,32},{7,160},{8,80},... | collective-permute-start | bytes 147464 | tf_op jit(solution)/shard_map/ppermute | solution.py:336
  32.3 6.5 %collective-permute-start.1 = (bf16[3,2,16,256]{3,2,1,0:T(8,128)(2,1)S(1)}, bf16[3,2,16,256]{3,2,1,0:T(8,128)(2,1)S(1)}, u32[]{:S(2)}, u32[]{:S(2)}) collective-permute-start(bf16[3,2,16,256]{3,2,1,0:T(8,128)(2,1)S(1)} %collective-permute-done), channel_id=1, source_target_pairs={{0,64},{16,80},{32,96},{48,112},{64,0},{80,16},{96,32},{112,48},{1... | collective-permute-start | bytes 147464 | tf_op jit(solution)/shard_map/ppermute | solution.py:319
  32.3 6.5 %collective-permute-start.2 = (bf16[3,2,16,256]{3,2,1,0:T(8,128)(2,1)S(1)}, bf16[3,2,16,256]{3,2,1,0:T(8,128)(2,1)S(1)}, u32[]{:S(2)}, u32[]{:S(2)}) collective-permute-start(bf16[3,2,16,256]{3,2,1,0:T(8,128)(2,1)S(1)} %collective-permute-done), channel_id=1, source_target_pairs={{0,128},{16,144},{32,160},{48,176},{64,192},{80,208},{96,224},{112... | collective-permute-start | bytes 147464 | tf_op jit(solution)/shard_map/ppermute | solution.py:319
  33.7 8.2 %collective-permute-start.3 = (bf16[3,2,16,256]{3,2,1,0:T(8,128)(2,1)S(1)}, bf16[3,2,16,256]{3,2,1,0:T(8,128)(2,1)S(1)}, u32[]{:S(2)}, u32[]{:S(2)}) collective-permute-start(bf16[3,2,16,256]{3,2,1,0:T(8,128)(2,1)S(1)} %collective-permute-done), channel_id=1, source_target_pairs={{0,192},{16,208},{32,224},{48,240},{64,128},{80,144},{96,160},{112... | collective-permute-start | bytes 147464 | tf_op jit(solution)/shard_map/ppermute | solution.py:319
  41.9 7.2 %collective-permute-start.4 = (bf16[4,3,2,16,256]{4,3,2,1,0:T(8,128)(2,1)S(1)}, bf16[4,3,2,16,256]{4,3,2,1,0:T(8,128)(2,1)S(1)}, u32[]{:S(2)}, u32[]{:S(2)}) collective-permute-start(bf16[4,3,2,16,256]{4,3,2,1,0:T(8,128)(2,1)S(1)} %get-tuple-element.20), channel_id=1, source_target_pairs={{0,32},{16,48},{32,0},{48,16},{64,96},{80,112},{96,64},{112,80},{1... | collective-permute-start | bytes 589832 | tf_op jit(solution)/shard_map/ppermute | solution.py:319
  49.1 1.9 %copy-start = (bf16[1,3,2,256,256]{4,3,2,1,0:T(8,128)(2,1)S(1)}, bf16[1,3,2,256,256]{4,3,2,1,0:T(8,128)(2,1)}, u32[]{:S(2)}) copy-start(bf16[1,3,2,256,256]{4,3,2,1,0:T(8,128)(2,1)} %param.10) | copy-start | bytes 2359300
  49.2 1.9 %copy-start.1 = (s32[256,256]{1,0:T(8,128)S(1)}, s32[256,256]{1,0:T(8,128)}, u32[]{:S(2)}) copy-start(s32[256,256]{1,0:T(8,128)} %keep_ref.1) | copy-start | bytes 786436
  49.2 1.9 %copy-start.2 = (bf16[256,768]{1,0:T(8,128)(2,1)S(1)}, bf16[256,768]{1,0:T(8,128)(2,1)}, u32[]{:S(2)}) copy-start(bf16[256,768]{1,0:T(8,128)(2,1)} %constant.22.clone.table_ref) | copy-start | bytes 1179652
  49.2 1.8 %collective-permute-start.5 = (bf16[8,3,2,16,256]{4,3,2,1,0:T(8,128)(2,1)S(1)}, bf16[8,3,2,16,256]{4,3,2,1,0:T(8,128)(2,1)S(1)}, u32[]{:S(2)}, u32[]{:S(2)}) collective-permute-start(bf16[8,3,2,16,256]{4,3,2,1,0:T(8,128)(2,1)S(1)} %bitcast.16), channel_id=1, source_target_pairs={{0,16},{16,0},{32,48},{48,32},{64,80},{80,64},{96,112},{112,96},{1... | collective-permute-start | bytes 1179656 | tf_op jit(solution)/shard_map/ppermute | solution.py:341
  54.0 2.1 %collective-permute-start.6 = (bf16[8,3,48,256]{3,2,1,0:T(8,128)(2,1)S(1)}, bf16[8,3,48,256]{3,2,1,0:T(8,128)(2,1)S(1)}, u32[]{:S(2)}, u32[]{:S(2)}) collective-permute-start(bf16[8,3,48,256]{3,2,1,0:T(8,128)(2,1)S(1)} %get-tuple-element.13), channel_id=1, source_target_pairs={{0,16},{16,0},{32,48},{48,32},{64,80},{80,64},{96,112},{112,96},{1... | collective-permute-start | bytes 1769480 | tf_op jit(solution)/shard_map/ppermute | solution.py:344
  72.5 4.2 %copy-start.4 = (bf16[32,32,3,3,3]{1,0,4,3,2:T(8,128)(2,1)S(1)}, bf16[32,32,3,3,3]{1,0,4,3,2:T(8,128)(2,1)}, u32[]{:S(2)}) copy-start(bf16[32,32,3,3,3]{1,0,4,3,2:T(8,128)(2,1)} %param.13) | copy-start | bytes 165892
  73.1 7.2 %collective-permute-start.7 = (bf16[3,48,256]{2,1,0:T(8,128)(2,1)S(1)}, bf16[3,48,256]{2,1,0:T(8,128)(2,1)S(1)}, u32[]{:S(2)}, u32[]{:S(2)}) collective-permute-start(bf16[3,48,256]{2,1,0:T(8,128)(2,1)S(1)} %get-tuple-element.14.own_ref), channel_id=1, source_target_pairs={{0,1},{1,2},{2,3},{3,4},{4,5},{5,6},{6,7},{7,8},{8,9},{9,10},{10,1... | collective-permute-start | bytes 221192 | tf_op jit(solution)/shard_map/ppermute | solution.py:349
  75.2 8.4 %collective-permute-start.8 = (bf16[3,48,256]{2,1,0:T(8,128)(2,1)S(1)}, bf16[3,48,256]{2,1,0:T(8,128)(2,1)S(1)}, u32[]{:S(2)}, u32[]{:S(2)}) collective-permute-start(bf16[3,48,256]{2,1,0:T(8,128)(2,1)S(1)} %get-tuple-element.14.own_ref), channel_id=1, source_target_pairs={{1,0},{2,1},{3,2},{4,3},{5,4},{6,5},{7,6},{8,7},{9,8},{10,9},{11,1... | collective-permute-start | bytes 221192 | tf_op jit(solution)/shard_map/ppermute | solution.py:350
  76.9 0.7 copy-start.5
  78.3 0.7 copy-start.6
  90.1 11.4 %collective-permute-start.9 = (bf16[3,2,16,256]{3,2,1,0:T(8,128)(2,1)S(1)}, bf16[3,2,16,256]{3,2,1,0:T(8,128)(2,1)S(1)}, u32[]{:S(2)}, u32[]{:S(2)}) collective-permute-start(bf16[3,2,16,256]{3,2,1,0:T(8,128)(2,1)S(1)} %regularized.1), channel_id=1, source_target_pairs={{64,0},{192,1},{96,2},{224,3},{0,4},{128,5},{32,6},{160,7},{80,8},... | collective-permute-start | bytes 147464 | tf_op jit(solution)/shard_map/ppermute | solution.py:352

commit v5 on v4

--- a/solution.py
+++ b/solution.py
@@ -242,13 +242,22 @@
     depth = 16
     size = 2 * depth
     w3 = w3_ref[:, :576]
-    terms = [dot(w3, a2_ref[x]) for x in range(rows + 2)]
+    last3 = rows - 1
+    terms = []
+    for x in range(rows + 2):
+        first, last = (max(x - last3, 0), min(x, 2))
+        value = dot(w3[first * 3 * size : (last + 1) * 3 * size], a2_ref[x])
+        terms.append((first, value))
     column3 = lax.broadcasted_iota(jnp.int32, (size, n), 1)
     for x in range(rows):
         sums = []
         for d in range(3):
-            at = lambda dx: (dx * 3 + d) * size
-            sums.append(sum(terms[x + dx][at(dx) : at(dx) + size] for dx in range(3)))
+            total = 0.0
+            for dx in range(3):
+                first, value = terms[x + dx]
+                at = ((dx - first) * 3 + d) * size
+                total = total + value[at : at + size]
+            sums.append(total)
         value = sums[1] + jnp.where(column3 == 0, 0.0, pltpu.roll(sums[0], 1, 1))
         value = value + jnp.where(column3 == n - 1, 0.0, pltpu.roll(sums[2], n - 1, 1))
         for p in range(2):

time: 104 us -> 104 us (level)
  no operation moved by 1% of the time
where the time goes in v5:
time: 104 us; the launch traced here: 102 us
  waiting for transfers between devices  38.7 us (37%)
  starting transfers between devices  32.3 us (31%)
  blocking collectives  16.3 us (16%)
  Pallas kernels  11.3 us (11%)
  local copies, waits for them, and re-layouts  2.36 us (2%)
    ppermute x1, waiting for transfers between devices, step(): brick = lax.ppermute(image.astype(BF16), ('coil', 'slab'), across)  18.9 us
    all_to_all x1, blocking collectives, step(): lax.all_to_all(terms, 'coil', 0, 0, tiled=True, axis_index_groups=chips)  16.3 us
    all_to_all x1, starting transfers between devices, step(): lax.all_to_all(sensitivity[0].reshape(slabs, rows, parts, depth, n), 'sla...  9.33 us
    ppermute x4, starting transfers between devices, gathered(): lax.ppermute(v, 'coil', [(i, i ^ 2 * k) for i in range(2 * chips)])  8.94 us
    ppermute x4, waiting for transfers between devices, gathered(): lax.ppermute(v, 'coil', [(i, i ^ 2 * k) for i in range(2 * chips)])  7.87 us
    pallas_call x1, Pallas kernels, regularized(): pl.pallas_call(conv_kernel, in_specs=[SMEM] + [VMEM] * 7, out_specs=VMEM,...  6.37 us
    ppermute x1, starting transfers between devices, step(): lax.ppermute(change, ('coil', 'slab'), [(c * slabs + a, a * slabs + b) fo...  6.25 us
    ppermute x1, waiting for transfers between devices, step(): lax.ppermute(change, ('coil', 'slab'), [(c * slabs + a, a * slabs + b) fo...  5.19 us
  transfers between devices with their start and end apart: 11, of which 7 were waited for; matrix products, arithmetic and copies ran while one was open for 1% of the time, Pallas kernels for 1%

profile of v5, /device:TPU:4, one launch (start us, length us, event | category | flops | bytes accessed | tf_op | source)
XLA Modules:
  0.0 102.1 jit_solution(4133655307393435136)
XLA Ops:
  0.0 0.0 copy-start.3
  0.0 9.3 %all-to-all-start = ((bf16[16,3,2,16,256]{4,3,2,1,0:T(8,128)(2,1)}), bf16[16,3,2,16,256]{4,3,2,1,0:T(8,128)(2,1)S(1)}, u32[]{:S(2)}, u32[]{:S(2)}) async-start(bf16[16,3,2,16,256]{4,3,2,1,0:T(8,128)(2,1)} %bitcast.20), calls=%async_computation | async-start | bytes 1572864 | tf_op jit(solution)/shard_map/all_to_all | solution.py:346
  9.3 0.0 copy-done.3
  9.4 4.0 %collective-permute-start = (bf16[3,2,16,256]{3,2,1,0:T(8,128)(2,1)S(1)}, bf16[3,2,16,256]{3,2,1,0:T(8,128)(2,1)S(1)}, u32[]{:S(2)}, u32[]{:S(2)}) collective-permute-start(bf16[3,2,16,256]{3,2,1,0:T(8,128)(2,1)S(1)} %convert_element_type.14), channel_id=1, source_target_pairs={{0,64},{1,192},{2,96},{3,224},{4,0},{5,128},{6,32},{7,160},{8,80},... | collective-permute-start | bytes 147464 | tf_op jit(solution)/shard_map/ppermute | solution.py:345
  13.3 18.9 %collective-permute-done = bf16[3,2,16,256]{3,2,1,0:T(8,128)(2,1)S(1)} collective-permute-done((bf16[3,2,16,256]{3,2,1,0:T(8,128)(2,1)S(1)}, bf16[3,2,16,256]{3,2,1,0:T(8,128)(2,1)S(1)}, u32[]{:S(2)}, u32[]{:S(2)}) %collective-permute-start) | collective-permute-done | bytes 49184 | tf_op jit(solution)/shard_map/ppermute | solution.py:345
  32.3 0.0 collective-permute-start.1
  32.3 1.4 %collective-permute-start.2 = (bf16[3,2,16,256]{3,2,1,0:T(8,128)(2,1)S(1)}, bf16[3,2,16,256]{3,2,1,0:T(8,128)(2,1)S(1)}, u32[]{:S(2)}, u32[]{:S(2)}) collective-permute-start(bf16[3,2,16,256]{3,2,1,0:T(8,128)(2,1)S(1)} %collective-permute-done), channel_id=1, source_target_pairs={{0,128},{16,144},{32,160},{48,176},{64,192},{80,208},{96,224},{112... | collective-permute-start | bytes 147464 | tf_op jit(solution)/shard_map/ppermute | solution.py:328
  33.7 5.1 %collective-permute-start.3 = (bf16[3,2,16,256]{3,2,1,0:T(8,128)(2,1)S(1)}, bf16[3,2,16,256]{3,2,1,0:T(8,128)(2,1)S(1)}, u32[]{:S(2)}, u32[]{:S(2)}) collective-permute-start(bf16[3,2,16,256]{3,2,1,0:T(8,128)(2,1)S(1)} %collective-permute-done), channel_id=1, source_target_pairs={{0,192},{16,208},{32,224},{48,240},{64,128},{80,144},{96,160},{112... | collective-permute-start | bytes 147464 | tf_op jit(solution)/shard_map/ppermute | solution.py:328
  38.8 0.0 collective-permute-done.1
  38.8 0.0 collective-permute-done.2
  38.8 3.1 %collective-permute-done.3 = bf16[3,2,16,256]{3,2,1,0:T(8,128)(2,1)S(1)} collective-permute-done((bf16[3,2,16,256]{3,2,1,0:T(8,128)(2,1)S(1)}, bf16[3,2,16,256]{3,2,1,0:T(8,128)(2,1)S(1)}, u32[]{:S(2)}, u32[]{:S(2)}) %collective-permute-start.3) | collective-permute-done | bytes 49184 | tf_op jit(solution)/shard_map/ppermute | solution.py:328
  41.9 2.4 %collective-permute-start.4 = (bf16[4,3,2,16,256]{4,3,2,1,0:T(8,128)(2,1)S(1)}, bf16[4,3,2,16,256]{4,3,2,1,0:T(8,128)(2,1)S(1)}, u32[]{:S(2)}, u32[]{:S(2)}) collective-permute-start(bf16[4,3,2,16,256]{4,3,2,1,0:T(8,128)(2,1)S(1)} %get-tuple-element.20), channel_id=1, source_target_pairs={{0,32},{16,48},{32,0},{48,16},{64,96},{80,112},{96,64},{112,80},{1... | collective-permute-start | bytes 589832 | tf_op jit(solution)/shard_map/ppermute | solution.py:328
  44.4 4.8 %collective-permute-done.4 = bf16[4,3,2,16,256]{4,3,2,1,0:T(8,128)(2,1)S(1)} collective-permute-done((bf16[4,3,2,16,256]{4,3,2,1,0:T(8,128)(2,1)S(1)}, bf16[4,3,2,16,256]{4,3,2,1,0:T(8,128)(2,1)S(1)}, u32[]{:S(2)}, u32[]{:S(2)}) %collective-permute-start.4) | collective-permute-done | bytes 196640 | tf_op jit(solution)/shard_map/ppermute | solution.py:328
  49.1 0.0 copy-start
  49.2 0.0 copy-start.1
  49.2 0.0 copy-start.2
  49.2 0.1 collective-permute-start.5
  49.3 0.1 pad_add_fusion.place_ref
  49.4 1.6 %collective-permute-done.5.img_b_ref = bf16[8,3,2,16,256]{4,3,2,1,0:T(8,128)(2,1)S(1)} collective-permute-done((bf16[8,3,2,16,256]{4,3,2,1,0:T(8,128)(2,1)S(1)}, bf16[8,3,2,16,256]{4,3,2,1,0:T(8,128)(2,1)S(1)}, u32[]{:S(2)}, u32[]{:S(2)}) %collective-permute-start.5) | collective-permute-done | bytes 393248 | tf_op jit(solution)/shard_map/ppermute | solution.py:350
  51.0 0.0 all-to-all-done.sens_ref
  51.0 0.0 copy-done
  51.0 0.0 copy-done.1
  51.0 0.0 copy-done.2
  51.0 3.0 %coil_terms.1 = (bf16[8,3,48,256]{3,2,1,0:T(8,128)(2,1)S(1)}, bf16[8,3,48,256]{3,2,1,0:T(8,128)(2,1)S(1)}) custom-call(s32[3]{0:T(128)S(1)} %pad_add_fusion.place_ref, bf16[16,3,2,16,256]{4,3,2,1,0:T(8,128)(2,1)S(1)} %all-to-all-done.sens_ref, bf16[8,3,2,16,256]{4,3,2,1,0:T(8,128)(2,1)S(1)} %bitcast.17, ...), custom_call_target="tpu_custom_call" | custom-call | flops 1610612736 | bytes 6291456 | tf_op jit(solution)/shard_map/coil_terms/pallas_call | solution.py:103
  54.0 0.2 collective-permute-start.6
  54.2 1.9 %collective-permute-done.6.b_ref = bf16[8,3,48,256]{3,2,1,0:T(8,128)(2,1)S(1)} collective-permute-done((bf16[8,3,48,256]{3,2,1,0:T(8,128)(2,1)S(1)}, bf16[8,3,48,256]{3,2,1,0:T(8,128)(2,1)S(1)}, u32[]{:S(2)}, u32[]{:S(2)}) %collective-permute-start.6) | collective-permute-done | bytes 589856 | tf_op jit(solution)/shard_map/ppermute | solution.py:353
  56.1 0.1 pair_sum.1
  56.2 16.3 %all_to_all.10.terms_ref = bf16[8,3,48,256]{3,2,1,0:T(8,128)(2,1)S(1)} all-to-all(bf16[8,3,48,256]{3,2,1,0:T(8,128)(2,1)S(1)} %pair_sum.1), channel_id=1, replica_groups={{0,32,64,96,128,160,192,224},{16,48,80,112,144,176,208,240},{1,33,65,97..., dimensions={0} | all-to-all | bytes 1179648 | tf_op jit(solution)/shard_map/all_to_all | solution.py:354
  72.5 0.0 copy-start.4
  72.5 0.7 start_brick.1
  73.1 2.1 %collective-permute-start.7 = (bf16[3,48,256]{2,1,0:T(8,128)(2,1)S(1)}, bf16[3,48,256]{2,1,0:T(8,128)(2,1)S(1)}, u32[]{:S(2)}, u32[]{:S(2)}) collective-permute-start(bf16[3,48,256]{2,1,0:T(8,128)(2,1)S(1)} %get-tuple-element.14.own_ref), channel_id=1, source_target_pairs={{0,1},{1,2},{2,3},{3,4},{4,5},{5,6},{6,7},{7,8},{8,9},{9,10},{10,1... | collective-permute-start | bytes 221192 | tf_op jit(solution)/shard_map/ppermute | solution.py:358
  75.2 1.5 %collective-permute-start.8 = (bf16[3,48,256]{2,1,0:T(8,128)(2,1)S(1)}, bf16[3,48,256]{2,1,0:T(8,128)(2,1)S(1)}, u32[]{:S(2)}, u32[]{:S(2)}) collective-permute-start(bf16[3,48,256]{2,1,0:T(8,128)(2,1)S(1)} %get-tuple-element.14.own_ref), channel_id=1, source_target_pairs={{1,0},{2,1},{3,2},{4,3},{5,4},{6,5},{7,6},{8,7},{9,8},{10,9},{11,1... | collective-permute-start | bytes 221192 | tf_op jit(solution)/shard_map/ppermute | solution.py:359
  76.7 0.0 copy-done.4
  76.7 0.2 copy.15
  76.9 0.0 copy-start.5
  76.9 0.2 reshape.14
  77.0 0.5 copy-done.5
  77.6 0.2 copy.17
  77.8 0.3 pad.16.clone
  78.1 0.1 reshape.13
  78.3 0.0 copy-start.6
  78.3 0.7 copy-done.6
  79.0 0.1 reshape.15
  79.1 1.3 %banded_weights.1 = (bf16[640,512]{1,0:T(8,128)(2,1)S(1)}, bf16[576,768]{1,0:T(8,128)(2,1)S(1)}, bf16[288,640]{1,0:T(8,128)(2,1)S(1)}) custom-call(bf16[32,512]{1,0:T(8,128)(2,1)S(1)} %pad.17.b1_ref, bf16[9,32,256]{2,1,0:T(8,128)(2,1)S(1)} %pad.18.b2_ref, bf16[18,640]{1,0:T(8,128)(2,1)S(1)} %pad.19.b3_ref), custom_call_target="tpu_custom_call" | custom-call | tf_op jit(solution)/shard_map/banded_weights/pallas_call | solution.py:313
  80.3 0.0 collective-permute-done.7.low_ref
  80.4 3.2 %collective-permute-done.8.high_ref = bf16[3,48,256]{2,1,0:T(8,128)(2,1)S(1)} collective-permute-done((bf16[3,48,256]{2,1,0:T(8,128)(2,1)S(1)}, bf16[3,48,256]{2,1,0:T(8,128)(2,1)S(1)}, u32[]{:S(2)}, u32[]{:S(2)}) %collective-permute-start.8) | collective-permute-done | bytes 73760 | tf_op jit(solution)/shard_map/ppermute | solution.py:359
  83.6 6.4 %regularized.1 = bf16[3,2,16,256]{3,2,1,0:T(8,128)(2,1)S(1)} custom-call(s32[3]{0:T(128)S(1)} %pad_add_fusion.place_ref, bf16[3,48,256]{2,1,0:T(8,128)(2,1)S(1)} %collective-permute-done.7.low_ref, bf16[3,48,256]{2,1,0:T(8,128)(2,1)S(1)} %get-tuple-element.14.own_ref, bf16[3,48,256]{2,1,0:T(8,128)(2,1)S(1)} %collective-permute-done.8.high_ref, ...), custom_call_target="tpu_custom_call" | custom-call | flops 6442450944 | bytes 4194304 | tf_op jit(solution)/shard_map/regularized/pallas_call | solution.py:270
  90.0 6.2 %collective-permute-start.9 = (bf16[3,2,16,256]{3,2,1,0:T(8,128)(2,1)S(1)}, bf16[3,2,16,256]{3,2,1,0:T(8,128)(2,1)S(1)}, u32[]{:S(2)}, u32[]{:S(2)}) collective-permute-start(bf16[3,2,16,256]{3,2,1,0:T(8,128)(2,1)S(1)} %regularized.1), channel_id=1, source_target_pairs={{64,0},{192,1},{96,2},{224,3},{0,4},{128,5},{32,6},{160,7},{80,8},... | collective-permute-start | bytes 147464 | tf_op jit(solution)/shard_map/ppermute | solution.py:361
  96.2 5.2 %collective-permute-done.9 = bf16[3,2,16,256]{3,2,1,0:T(8,128)(2,1)S(1)} collective-permute-done((bf16[3,2,16,256]{3,2,1,0:T(8,128)(2,1)S(1)}, bf16[3,2,16,256]{3,2,1,0:T(8,128)(2,1)S(1)}, u32[]{:S(2)}, u32[]{:S(2)}) %collective-permute-start.9) | collective-permute-done | bytes 49184 | tf_op jit(solution)/shard_map/ppermute | solution.py:361
  101.4 0.7 convert_add_fusion
  (8 shorter events, 0.2 us)
Async XLA Ops:
  0.0 9.3 %copy-start.3 = (f32[3,2,16,256]{3,2,1,0:T(8,128)S(1)}, f32[3,2,16,256]{3,2,1,0:T(8,128)}, u32[]{:S(2)}) copy-start(f32[3,2,16,256]{3,2,1,0:T(8,128)} %param.8) | copy-start | bytes 294916
  0.0 51.0 %all-to-all-start = ((bf16[16,3,2,16,256]{4,3,2,1,0:T(8,128)(2,1)}), bf16[16,3,2,16,256]{4,3,2,1,0:T(8,128)(2,1)S(1)}, u32[]{:S(2)}, u32[]{:S(2)}) async-start(bf16[16,3,2,16,256]{4,3,2,1,0:T(8,128)(2,1)} %bitcast.20), calls=%async_computation | async-start | bytes 1572864 | tf_op jit(solution)/shard_map/all_to_all | solution.py:346
  9.4 22.9 %collective-permute-start = (bf16[3,2,16,256]{3,2,1,0:T(8,128)(2,1)S(1)}, bf16[3,2,16,256]{3,2,1,0:T(8,128)(2,1)S(1)}, u32[]{:S(2)}, u32[]{:S(2)}) collective-permute-start(bf16[3,2,16,256]{3,2,1,0:T(8,128)(2,1)S(1)} %convert_element_type.14), channel_id=1, source_target_pairs={{0,64},{1,192},{2,96},{3,224},{4,0},{5,128},{6,32},{7,160},{8,80},... | collective-permute-start | bytes 147464 | tf_op jit(solution)/shard_map/ppermute | solution.py:345
  32.3 6.5 %collective-permute-start.1 = (bf16[3,2,16,256]{3,2,1,0:T(8,128)(2,1)S(1)}, bf16[3,2,16,256]{3,2,1,0:T(8,128)(2,1)S(1)}, u32[]{:S(2)}, u32[]{:S(2)}) collective-permute-start(bf16[3,2,16,256]{3,2,1,0:T(8,128)(2,1)S(1)} %collective-permute-done), channel_id=1, source_target_pairs={{0,64},{16,80},{32,96},{48,112},{64,0},{80,16},{96,32},{112,48},{1... | collective-permute-start | bytes 147464 | tf_op jit(solution)/shard_map/ppermute | solution.py:328
  32.3 6.5 %collective-permute-start.2 = (bf16[3,2,16,256]{3,2,1,0:T(8,128)(2,1)S(1)}, bf16[3,2,16,256]{3,2,1,0:T(8,128)(2,1)S(1)}, u32[]{:S(2)}, u32[]{:S(2)}) collective-permute-start(bf16[3,2,16,256]{3,2,1,0:T(8,128)(2,1)S(1)} %collective-permute-done), channel_id=1, source_target_pairs={{0,128},{16,144},{32,160},{48,176},{64,192},{80,208},{96,224},{112... | collective-permute-start | bytes 147464 | tf_op jit(solution)/shard_map/ppermute | solution.py:328
  33.7 8.2 %collective-permute-start.3 = (bf16[3,2,16,256]{3,2,1,0:T(8,128)(2,1)S(1)}, bf16[3,2,16,256]{3,2,1,0:T(8,128)(2,1)S(1)}, u32[]{:S(2)}, u32[]{:S(2)}) collective-permute-start(bf16[3,2,16,256]{3,2,1,0:T(8,128)(2,1)S(1)} %collective-permute-done), channel_id=1, source_target_pairs={{0,192},{16,208},{32,224},{48,240},{64,128},{80,144},{96,160},{112... | collective-permute-start | bytes 147464 | tf_op jit(solution)/shard_map/ppermute | solution.py:328
  41.9 7.2 %collective-permute-start.4 = (bf16[4,3,2,16,256]{4,3,2,1,0:T(8,128)(2,1)S(1)}, bf16[4,3,2,16,256]{4,3,2,1,0:T(8,128)(2,1)S(1)}, u32[]{:S(2)}, u32[]{:S(2)}) collective-permute-start(bf16[4,3,2,16,256]{4,3,2,1,0:T(8,128)(2,1)S(1)} %get-tuple-element.20), channel_id=1, source_target_pairs={{0,32},{16,48},{32,0},{48,16},{64,96},{80,112},{96,64},{112,80},{1... | collective-permute-start | bytes 589832 | tf_op jit(solution)/shard_map/ppermute | solution.py:328
  49.1 1.9 %copy-start = (bf16[1,3,2,256,256]{4,3,2,1,0:T(8,128)(2,1)S(1)}, bf16[1,3,2,256,256]{4,3,2,1,0:T(8,128)(2,1)}, u32[]{:S(2)}) copy-start(bf16[1,3,2,256,256]{4,3,2,1,0:T(8,128)(2,1)} %param.10) | copy-start | bytes 2359300
  49.2 1.9 %copy-start.1 = (s32[256,256]{1,0:T(8,128)S(1)}, s32[256,256]{1,0:T(8,128)}, u32[]{:S(2)}) copy-start(s32[256,256]{1,0:T(8,128)} %keep_ref.1) | copy-start | bytes 786436
  49.2 1.9 %copy-start.2 = (bf16[256,768]{1,0:T(8,128)(2,1)S(1)}, bf16[256,768]{1,0:T(8,128)(2,1)}, u32[]{:S(2)}) copy-start(bf16[256,768]{1,0:T(8,128)(2,1)} %constant.22.clone.table_ref) | copy-start | bytes 1179652
  49.2 1.8 %collective-permute-start.5 = (bf16[8,3,2,16,256]{4,3,2,1,0:T(8,128)(2,1)S(1)}, bf16[8,3,2,16,256]{4,3,2,1,0:T(8,128)(2,1)S(1)}, u32[]{:S(2)}, u32[]{:S(2)}) collective-permute-start(bf16[8,3,2,16,256]{4,3,2,1,0:T(8,128)(2,1)S(1)} %bitcast.16), channel_id=1, source_target_pairs={{0,16},{16,0},{32,48},{48,32},{64,80},{80,64},{96,112},{112,96},{1... | collective-permute-start | bytes 1179656 | tf_op jit(solution)/shard_map/ppermute | solution.py:350
  54.0 2.1 %collective-permute-start.6 = (bf16[8,3,48,256]{3,2,1,0:T(8,128)(2,1)S(1)}, bf16[8,3,48,256]{3,2,1,0:T(8,128)(2,1)S(1)}, u32[]{:S(2)}, u32[]{:S(2)}) collective-permute-start(bf16[8,3,48,256]{3,2,1,0:T(8,128)(2,1)S(1)} %get-tuple-element.13), channel_id=1, source_target_pairs={{0,16},{16,0},{32,48},{48,32},{64,80},{80,64},{96,112},{112,96},{1... | collective-permute-start | bytes 1769480 | tf_op jit(solution)/shard_map/ppermute | solution.py:353
  72.5 4.2 %copy-start.4 = (bf16[32,32,3,3,3]{1,0,4,3,2:T(8,128)(2,1)S(1)}, bf16[32,32,3,3,3]{1,0,4,3,2:T(8,128)(2,1)}, u32[]{:S(2)}) copy-start(bf16[32,32,3,3,3]{1,0,4,3,2:T(8,128)(2,1)} %param.13) | copy-start | bytes 165892
  73.1 7.2 %collective-permute-start.7 = (bf16[3,48,256]{2,1,0:T(8,128)(2,1)S(1)}, bf16[3,48,256]{2,1,0:T(8,128)(2,1)S(1)}, u32[]{:S(2)}, u32[]{:S(2)}) collective-permute-start(bf16[3,48,256]{2,1,0:T(8,128)(2,1)S(1)} %get-tuple-element.14.own_ref), channel_id=1, source_target_pairs={{0,1},{1,2},{2,3},{3,4},{4,5},{5,6},{6,7},{7,8},{8,9},{9,10},{10,1... | collective-permute-start | bytes 221192 | tf_op jit(solution)/shard_map/ppermute | solution.py:358
  75.2 8.4 %collective-permute-start.8 = (bf16[3,48,256]{2,1,0:T(8,128)(2,1)S(1)}, bf16[3,48,256]{2,1,0:T(8,128)(2,1)S(1)}, u32[]{:S(2)}, u32[]{:S(2)}) collective-permute-start(bf16[3,48,256]{2,1,0:T(8,128)(2,1)S(1)} %get-tuple-element.14.own_ref), channel_id=1, source_target_pairs={{1,0},{2,1},{3,2},{4,3},{5,4},{6,5},{7,6},{8,7},{9,8},{10,9},{11,1... | collective-permute-start | bytes 221192 | tf_op jit(solution)/shard_map/ppermute | solution.py:359
  76.9 0.7 copy-start.5
  78.3 0.7 copy-start.6
  90.0 11.4 %collective-permute-start.9 = (bf16[3,2,16,256]{3,2,1,0:T(8,128)(2,1)S(1)}, bf16[3,2,16,256]{3,2,1,0:T(8,128)(2,1)S(1)}, u32[]{:S(2)}, u32[]{:S(2)}) collective-permute-start(bf16[3,2,16,256]{3,2,1,0:T(8,128)(2,1)S(1)} %regularized.1), channel_id=1, source_target_pairs={{64,0},{192,1},{96,2},{224,3},{0,4},{128,5},{32,6},{160,7},{80,8},... | collective-permute-start | bytes 147464 | tf_op jit(solution)/shard_map/ppermute | solution.py:361
